TPU v7x, 256 devices: a whole 4x4x8 slice. The times are simulated.
256 devices in a mesh: tm: 4 (over y), mp: 4 (over x_hi, core), section: 16 (over z, x_lo).
Axes of the slice: x: 4 (x_hi: 2, x_lo: 2; x = x_hi * 2 + x_lo), y: 4, z: 8, core: 2. Of those that a mesh axis runs over, the one named last changes fastest.
Arguments:
- mel_frames: bfloat16 [32768, 128], P(('tm', 'section')), may hold values from -6 to 6
- conv1_weight: bfloat16 [3, 128, 1280], P(None, None, 'mp'), may hold values from -0.3125 to 0.3125
- conv2_weight: bfloat16 [3, 1280, 1280], P(None, 'section', 'mp'), may hold values from -0.09375 to 0.09375
- attn_gain: float32 [1280], P('mp'), may hold values from 0.1 to 1.9
- qkv_weight: bfloat16 [1280, 3, 1024], P('section', None, 'mp')
- out_weight: bfloat16 [1024, 1280], P('mp'), may hold values from -0.1875 to 0.1875
- post_gain: float32 [1280], P('mp'), may hold values from 0.1 to 1.9
- proj_weight: bfloat16 [1280, 4096], P('section', 'mp'), may hold values from -0.15625 to 0.15625
- rms_gain: float32 [4096], P('mp'), may hold values from 0.1 to 1.9
- kv_weight: bfloat16 [4096, 4096], P(('mp', 'section')), may hold values from -0.09375 to 0.09375
Outputs:
- kv_cache: bfloat16 [8192, 4096], P(('tm', 'section'), 'mp')
All inputs are finite; a program needn't handle non-finite values.
Results may differ from a plain program's by a relative error of at most 0.04.
Values may be sent and summed in bfloat16 or wider, within the bound.
A program may use at most 64 MiB of HBM per device.

v0:
```python
import math

import jax
import jax.numpy as jnp
from jax import lax
from jax.sharding import PartitionSpec as P

D = 1280
HD = 64
DL = 4096
KVH = 16
LHD = 128


def extended_2(cells, sides, width):
    for axis, dim in sides:
        count = lax.axis_size(axis)
        ends = count - 1
        head = lax.slice_in_dim(cells, 0, width, axis=dim)
        tail = lax.slice_in_dim(cells, cells.shape[dim] - width, cells.shape[dim], axis=dim)
        cells = jnp.concatenate(
            [
                lax.ppermute(tail, axis, [(i, (i + 1) % count) for i in range(ends)]),
                cells,
                lax.ppermute(head, axis, [((i + 1) % count, i) for i in range(ends)]),
            ],
            axis=dim,
        )
    return cells


def shifted(value, axis, steps):
    count = lax.axis_size(axis)
    initial, last = (max(0, -steps), min(count, count - steps))
    return lax.ppermute(value, axis, [(source, source + steps) for source in range(initial, last)])


def exact_gelu(values):
    return jax.nn.gelu(values, approximate=False)


def spread_norm(rows, gain):
    sum_rows, sum_squares = lax.psum((jnp.sum(rows, axis=-1), jnp.sum(rows * rows, axis=-1)), "mp")
    center = sum_rows / D
    spread = sum_squares / D - center * center
    return (rows - center[:, None]) * lax.rsqrt(spread[:, None] + 1e-05) * gain


def rotate_keys(cache, row_start, col_start):
    rows_count, cols_count = cache.shape
    positions = (row_start + jnp.arange(rows_count, dtype=jnp.int32)).astype(jnp.float32)
    columns = col_start + jnp.arange(cols_count, dtype=jnp.int32)
    half_size = LHD // 2
    within = columns % LHD % half_size
    freq = jnp.power(10000.0, -2.0 * within.astype(jnp.float32) / LHD)
    angle = positions[:, None] * freq[None, :]
    grouped = cache.reshape(rows_count, cols_count // LHD, 2, half_size)
    partner = jnp.stack([-grouped[:, :, 1], grouped[:, :, 0]], axis=2).reshape(
        rows_count, cols_count
    )
    turned = cache * jnp.cos(angle) + partner * jnp.sin(angle)
    return jnp.where((columns < KVH * LHD)[None, :], turned, cache)


def attend_block(state, pairs, queries):
    peak, weight_sum, output = state
    heads = queries.shape[1]
    width = heads * HD
    length = pairs.shape[0]
    keys_part = pairs[:, :width].reshape(length, heads, HD)
    values_part = pairs[:, width:].reshape(length, heads, HD)
    scores = (
        jnp.einsum("qhd,khd->hqk", queries, keys_part, preferred_element_type=jnp.float32) * 0.125
    )
    fresh = jnp.maximum(peak, jnp.max(scores, axis=-1))
    decay = jnp.exp(peak - fresh)
    weights = jnp.exp(scores - fresh[:, :, None])
    weight_sum = weight_sum * decay + jnp.sum(weights, axis=-1)
    product = jnp.einsum(
        "hqk,khd->qhd",
        weights.astype(jnp.bfloat16),
        values_part,
        preferred_element_type=jnp.float32,
    )
    output = output * jnp.transpose(decay)[:, :, None] + product
    return (fresh, weight_sum, output)


def fold_keys(queries, state, piece):
    length = piece.shape[0]
    step_rows = math.gcd(length, 512)

    def advance(index, inner):
        pairs = lax.dynamic_slice_in_dim(piece, index * step_rows, step_rows, 0)
        return attend_block(inner, pairs, queries)

    return lax.fori_loop(0, length // step_rows, advance, state)


def start_state(heads, count):
    return (
        jnp.full((heads, count), -1e30, jnp.float32),
        jnp.zeros((heads, count), jnp.float32),
        jnp.zeros((count, heads, HD), jnp.float32),
    )


def shards(
    mel_frames,
    conv1_weight,
    conv2_weight,
    attn_gain,
    qkv_weight,
    out_weight,
    post_gain,
    proj_weight,
    rms_gain,
    kv_weight,
):
    conv2_full, qkv_full, proj_full, kv_full = (
        lax.all_gather(conv2_weight, "section", axis=1, tiled=True),
        lax.all_gather(qkv_weight, "section", axis=0, tiled=True),
        lax.all_gather(proj_weight, "section", axis=0, tiled=True),
        lax.all_gather(kv_weight, "section", axis=0, tiled=True),
    )
    frames_local = mel_frames.shape[0]
    encoded = frames_local // 2
    channels = conv1_weight.shape[2]
    padded = extended_2(mel_frames, ((("tm", "section"), 0),), 1)
    first_sum = jnp.dot(padded[0:frames_local], conv1_weight[0], preferred_element_type=jnp.float32)
    first_sum = first_sum + jnp.dot(
        padded[1 : frames_local + 1], conv1_weight[1], preferred_element_type=jnp.float32
    )
    first_sum = first_sum + jnp.dot(
        padded[2 : frames_local + 2], conv1_weight[2], preferred_element_type=jnp.float32
    )
    first = exact_gelu(first_sum).astype(jnp.bfloat16)
    before = shifted(first[frames_local - 1 :], ("tm", "section"), 1)
    extended = jnp.concatenate([before, first], axis=0)
    piece = lax.all_gather(extended, "mp", axis=1, tiled=True)
    state = jnp.dot(piece[0:frames_local:2], conv2_full[0], preferred_element_type=jnp.float32)
    state = state + jnp.dot(
        piece[1 : frames_local + 1 : 2], conv2_full[1], preferred_element_type=jnp.float32
    )
    second = state + jnp.dot(
        piece[2 : frames_local + 2 : 2], conv2_full[2], preferred_element_type=jnp.float32
    )
    hidden = exact_gelu(second).astype(jnp.bfloat16)
    normed = spread_norm(hidden.astype(jnp.float32), attn_gain).astype(jnp.bfloat16)
    qkv_cols = qkv_full.shape[1] * qkv_full.shape[2]
    piece = lax.all_gather(normed, "mp", axis=1, tiled=True)
    weight_rows = qkv_full.reshape(piece.shape[1], qkv_cols)
    projected = jnp.dot(piece, weight_rows, preferred_element_type=jnp.float32).astype(jnp.bfloat16)
    width = qkv_full.shape[2]
    heads = width // HD
    queries = projected[:, :width].reshape(encoded, heads, HD)
    pairs = projected[:, width:]
    peak, weight_sum, output = fold_keys(
        queries,
        start_state(heads, encoded),
        lax.all_gather(pairs, ("tm", "section"), axis=0, tiled=True),
    )
    attended = (
        (output / jnp.transpose(weight_sum)[:, :, None])
        .astype(jnp.bfloat16)
        .reshape(encoded, width)
    )
    mixed = lax.psum_scatter(
        jnp.dot(attended, out_weight, preferred_element_type=jnp.float32).astype(jnp.bfloat16),
        "mp",
        scatter_dimension=1,
        tiled=True,
    ).astype(jnp.float32)
    residual = hidden.astype(jnp.float32) + mixed
    pooled_rows = encoded // 2
    pooled = jnp.mean(residual.reshape(pooled_rows, 2, channels), axis=1)
    post = spread_norm(pooled, post_gain).astype(jnp.bfloat16)
    weight_rows = proj_full
    embedded = jnp.dot(
        lax.all_gather(post, "mp", axis=1, tiled=True),
        weight_rows,
        preferred_element_type=jnp.float32,
    ).astype(jnp.bfloat16)
    widened = embedded.astype(jnp.float32)
    squares = lax.psum(jnp.sum(widened * widened, axis=-1), "mp")
    scaled = (widened * lax.rsqrt(squares[:, None] / DL + 1e-06) * rms_gain).astype(jnp.bfloat16)
    cache = lax.psum_scatter(
        jnp.dot(scaled, kv_full, preferred_element_type=jnp.float32).astype(jnp.bfloat16),
        "mp",
        scatter_dimension=1,
        tiled=True,
    ).astype(jnp.float32)
    row_start = (
        lax.axis_index("tm") * lax.axis_size("section") + lax.axis_index("section")
    ) * pooled_rows
    col_start = lax.axis_index("mp") * cache.shape[1]
    return rotate_keys(cache, row_start, col_start).astype(jnp.bfloat16)


def solution(mesh):
    return jax.shard_map(
        shards,
        mesh=mesh,
        in_specs=(
            P(("tm", "section"), None),
            P(None, None, "mp"),
            P(None, "section", "mp"),
            P("mp"),
            P("section", None, "mp"),
            P("mp", None),
            P("mp"),
            P("section", "mp"),
            P("mp"),
            P(("mp", "section"), None),
        ),
        out_specs=P(("tm", "section"), "mp"),
        check_vma=False,
    )
```

profile of v0, /device:TPU:1, one launch (start us, length us, event | category | flops | bytes accessed | tf_op | source)
XLA Modules:
  0.0 1095.8 jit_solution(13672891319570024660)
XLA Ops:
  8.6 4.6 collective-permute-start
  15.6 2.5 fusion.15
  18.2 4.3 collective-permute-start.2
  22.5 1.5 collective-permute-done.2
  26.7 34.7 %all-gather.18.cloned.1.call-done = bf16[4,320,513]{1,2,0:T(8,128)(2,1)} async-done(((bf16[1,320,513]{1,2,0:T(8,128)(2,1)}), bf16[4,320,513]{1,2,0:T(8,128)(2,1)}) %all-gather.18.cloned.1.call-update) | async-done | bytes 1313296 | tf_op jit(solution)/shard_map/all_gather | solution.py:140
  61.4 3.2 copy.40
  64.5 3.1 reshape.94
  70.0 4.3 slice.82
  74.4 49.4 %all-gather.10.cloned.1.call-done = bf16[1280,3,256]{2,0,1:T(8,128)(2,1)} async-done(((bf16[80,3,256]{2,0,1:T(8,128)(2,1)}), bf16[1280,3,256]{2,0,1:T(8,128)(2,1)}) %all-gather.10.cloned.1.call-update) | async-done | bytes 1966096 | tf_op jit(solution)/shard_map/all_gather | solution.py:122
  123.8 4.0 copy.41
  127.8 80.1 %all-gather.8.cloned.1.call-done = bf16[3,1280,320]{2,1,0:T(8,128)(2,1)} async-done(((bf16[3,80,320]{2,1,0:T(8,128)(2,1)}), bf16[3,1280,320]{2,1,0:T(8,128)(2,1)}) %all-gather.8.cloned.1.call-update) | async-done | bytes 2457616 | tf_op jit(solution)/shard_map/all_gather | solution.py:121
  207.9 1.8 fusion.12
  209.7 1.7 convolution_add_fusion.2
  211.4 2.6 convert_reduce_fusion
  214.0 13.5 %all-reduce.1 = (f32[256]{0:T(256)S(1)}, f32[256]{0:T(256)S(1)}) all-reduce(f32[256]{0:T(256)S(1)} %get-tuple-element.171, f32[256]{0:T(256)S(1)} %get-tuple-element.170), channel_id=1, replica_groups=mesh['tm'=4,'mp'=4,'section'=16] {'mp'}, use_global_device_ids=true, to_apply=%region_3.0 | all-reduce | flops 512 | bytes 4096 | tf_op jit(solution)/shard_map/psum | solution.py:43
  227.6 10.1 all_gather.26
  240.1 367.4 %all-gather.12.cloned.1.call-done = bf16[16384,512]{1,0:T(8,128)(2,1)} async-done(((bf16[256,512]{1,0:T(8,128)(2,1)}), bf16[16384,512]{1,0:T(8,128)(2,1)}) %all-gather.12.cloned.1.call-update) | async-done | bytes 16777232 | tf_op jit(solution)/shard_map/all_gather | solution.py:161
  607.5 137.7 %while.18 = (s32[]{:T(128)}, f32[4,256]{1,0:T(4,128)S(1)}, f32[4,256]{1,0:T(4,128)}, f32[256,4,64]{0,2,1:T(8,128)S(1)}, bf16[16384,512]{1,0:T(8,128)(2,1)}, /*in...) while((s32[]{:T(128)}, f32[4,256]{1,0:T(4,128)S(1)}, ...), condition=%wide.region_7.0_spmd.clone, body=%wide.region_4.0_spmd.clone.sunk | while | flops 138614784 | bytes 9666803 | solution.py:97
  638.8 1.4 bitcast_reduce_fusion.2
  643.1 1.4 bitcast_reduce_fusion.2
  647.5 1.4 bitcast_reduce_fusion.2
  677.6 1.4 bitcast_reduce_fusion.2
  748.6 32.9 %reduce-scatter.3.cloned.1.call-done = bf16[256,320]{0,1:T(8,128)(2,1)} async-done(((bf16[256,1280]{0,1:T(8,128)(2,1)}), bf16[256,320]{0,1:T(8,128)(2,1)}) %reduce-scatter.3.cloned.1.call-update) | async-done | bytes 163856 | tf_op jit(solution)/shard_map/reduce_scatter | solution.py:168
  783.4 7.5 all-reduce
  791.2 11.0 %all_gather.29 = bf16[128,1280]{0,1:T(8,128)(2,1)S(1)} all-gather(bf16[128,320]{0,1:T(8,128)(2,1)S(1)} %copy.45), channel_id=1, replica_groups=mesh['tm'=4,'mp'=4,'section'=16] {'mp'}, dimensions={1}, use_global_device_ids=true | all-gather | bytes 409600 | tf_op jit(solution)/shard_map/all_gather | solution.py:180
  802.2 49.2 %all-gather.14.cloned.1.call-done = bf16[1280,1024]{1,0:T(8,128)(2,1)} async-done(((bf16[80,1024]{1,0:T(8,128)(2,1)}), bf16[1280,1024]{1,0:T(8,128)(2,1)}) %all-gather.14.cloned.1.call-update) | async-done | bytes 2621456 | tf_op jit(solution)/shard_map/all_gather | solution.py:123
  851.4 2.4 multiply_reduce_fusion
  853.7 14.9 %psum.39 = f32[128]{0:T(128)S(1)} all-reduce(f32[128]{0:T(128)S(1)} %get-tuple-element.203), channel_id=1, replica_groups=mesh['tm'=4,'mp'=4,'section'=16] {'mp'}, use_global_device_ids=true, to_apply=%region_15.0 | all-reduce | flops 128 | bytes 1024 | tf_op jit(solution)/shard_map/psum | solution.py:185
  868.7 172.2 %all-gather.16.cloned.1.call-done = bf16[1024,4096]{1,0:T(8,128)(2,1)} async-done(((bf16[64,4096]{1,0:T(8,128)(2,1)}), bf16[1024,4096]{1,0:T(8,128)(2,1)}) %all-gather.16.cloned.1.call-update) | async-done | bytes 8388624 | tf_op jit(solution)/shard_map/all_gather | solution.py:124
  1040.9 5.7 convolution_convert_fusion
  1046.7 37.8 %reduce-scatter.5.cloned.1.call-done = bf16[128,1024]{1,0:T(8,128)(2,1)} async-done(((bf16[128,4096]{1,0:T(8,128)(2,1)}), bf16[128,1024]{1,0:T(8,128)(2,1)}) %reduce-scatter.5.cloned.1.call-update) | async-done | bytes 262160 | tf_op jit(solution)/shard_map/reduce_scatter | solution.py:187
  1086.0 3.0 fusion.26
  (484 shorter events, 148.6 us)
Async XLA Ops:
  6.5 739.4 %copy-start = (bf16[256,1280]{1,0:T(8,128)(2,1)S(1)}, bf16[256,1280]{1,0:T(8,128)(2,1)}, u32[]{:S(2)}) copy-start(bf16[256,1280]{1,0:T(8,128)(2,1)} %param.17) | copy-start | bytes 1966084
  6.5 54.8 %all-gather.18.cloned.1.call-start = ((), (), s32[]{:S(2)}) async-start(), calls=%async_computation.9 | async-start | bytes 1996800 | tf_op jit(solution)/shard_map/all_gather | solution.py:140
  7.3 7.1 collective-permute-start.1
  8.6 7.0 collective-permute-start
  18.2 5.7 collective-permute-start.2
  25.1 98.7 %all-gather.10.cloned.1.call-start = ((), (), s32[]{:S(2)}) async-start(), calls=%async_computation.3 | async-start | bytes 2088960 | tf_op jit(solution)/shard_map/all_gather | solution.py:122
  25.9 182.0 %all-gather.8.cloned.1.call-start = ((), (), s32[]{:S(2)}) async-start(), calls=%async_computation.2 | async-start | bytes 3133440 | tf_op jit(solution)/shard_map/all_gather | solution.py:121
  26.6 580.9 %all-gather.12.cloned.1.call-start = ((), (), s32[]{:S(2)}) async-start(), calls=%async_computation.4 | async-start | bytes 17039360 | tf_op jit(solution)/shard_map/all_gather | solution.py:161
  207.9 3.5 copy-start.3
  211.4 16.1 %copy-start.10 = (f32[320]{0:T(512)S(1)}, f32[320]{0:T(512)}, u32[]{:S(2)}) copy-start(f32[320]{0:T(512)} %param.15) | copy-start | bytes 3844
  211.4 26.3 %copy-start.1 = (bf16[1280,3,256]{0,2,1:T(8,128)(2,1)S(1)}, bf16[1280,3,256]{0,2,1:T(8,128)(2,1)}, u32[]{:S(2)}) copy-start(bf16[1280,3,256]{0,2,1:T(8,128)(2,1)} %copy.41) | copy-start | bytes 5898244
  214.0 24.5 %copy-start.4 = (bf16[256,320]{0,1:T(8,128)(2,1)}, bf16[256,320]{0,1:T(8,128)(2,1)S(1)}, u32[]{:S(2)}) copy-start(bf16[256,320]{0,1:T(8,128)(2,1)S(1)} %get-tuple-element.202) | copy-start | bytes 491524
  239.2 542.3 %reduce-scatter.3.cloned.1.call-start = ((), (), s32[]{:S(2)}) async-start(), calls=%async_computation.5 | async-start | bytes 819200 | tf_op jit(solution)/shard_map/reduce_scatter | solution.py:168
  614.6 0.9 copy-start.6
  618.9 0.9 copy-start.6
  623.2 0.9 copy-start.6
  627.5 0.9 copy-start.6
  649.0 0.9 copy-start.6
  653.3 0.9 copy-start.6
  657.6 0.9 copy-start.6
  661.9 0.9 copy-start.6
  666.2 0.9 copy-start.6
  670.5 0.9 copy-start.6
  692.1 0.9 copy-start.6
  696.4 0.9 copy-start.6
  745.2 36.3 %copy-start.5 = (bf16[256,320]{0,1:T(8,128)(2,1)S(1)}, bf16[256,320]{0,1:T(8,128)(2,1)}, u32[]{:S(2)}) copy-start(bf16[256,320]{0,1:T(8,128)(2,1)} %copy-done.4) | copy-start | bytes 491524
  747.2 43.8 %copy-start.9 = (f32[320]{0:T(512)S(1)}, f32[320]{0:T(512)}, u32[]{:S(2)}) copy-start(f32[320]{0:T(512)} %param.18) | copy-start | bytes 3844
  747.2 104.2 %all-gather.14.cloned.1.call-start = ((), (), s32[]{:S(2)}) async-start(), calls=%async_computation.6 | async-start | bytes 2785280 | tf_op jit(solution)/shard_map/all_gather | solution.py:123
  747.8 293.1 %all-gather.16.cloned.1.call-start = ((), (), s32[]{:S(2)}) async-start(), calls=%async_computation.7 | async-start | bytes 8912896 | tf_op jit(solution)/shard_map/all_gather | solution.py:124
  748.6 335.9 %reduce-scatter.5.cloned.1.call-start = ((), (), s32[]{:S(2)}) async-start(), calls=%async_computation.8 | async-start | bytes 1310720 | tf_op jit(solution)/shard_map/reduce_scatter | solution.py:187
  791.1 249.8 %copy-start.8 = (f32[1024]{0:T(1024)S(1)}, f32[1024]{0:T(1024)}, u32[]{:S(2)}) copy-start(f32[1024]{0:T(1024)} %param.20) | copy-start | bytes 12292
  1084.5 1.5 copy-start.2
  (52 other events, 36.9 us)
Sparse Core Ops, SparseCore 0:
  25.3 36.0 all-gather.17
  63.2 60.5 all-gather.9
  125.6 82.2 all-gather.7
  239.3 368.1 all-gather.11
  747.3 34.0 reduce-scatter.2
  783.1 68.2 all-gather.13
  853.2 187.6 all-gather.15
  1046.8 37.6 reduce-scatter.4
where the time goes:
time: 1100 us
  waiting for transfers between devices  828 us (75%)
  local copies, waits for them, and re-layouts  83.7 us (8%)
  matrix products  82.1 us (7%)
  blocking collectives  57 us (5%)
  other arithmetic  18.3 us (2%)
  between operations  13.8 us (1%)
    all_gather x1, waiting for transfers between devices, shards(): lax.all_gather(pairs, ('tm', 'section'), axis=0, tiled=True)  367 us
    all_gather x1, waiting for transfers between devices, shards(): lax.all_gather(kv_weight, 'section', axis=0, tiled=True)  172 us
    all_gather x1, waiting for transfers between devices, shards(): lax.all_gather(conv2_weight, 'section', axis=1, tiled=True)  80.1 us
    all_gather x1, waiting for transfers between devices, shards(): lax.all_gather(qkv_weight, 'section', axis=0, tiled=True)  49.4 us
    all_gather x1, waiting for transfers between devices, shards(): lax.all_gather(proj_weight, 'section', axis=0, tiled=True)  49.2 us
    dot_general x32, matrix products, attend_block(): jnp.einsum('qhd,khd->hqk', queries, keys_part, preferred_element_type=jnp...  44.8 us
    reduce_scatter x1, waiting for transfers between devices, shards(): lax.psum_scatter(jnp.dot(scaled, kv_full, preferred_element_type=jnp.floa...  37.8 us
    all_gather x1, waiting for transfers between devices, shards(): piece = lax.all_gather(extended, 'mp', axis=1, tiled=True)  34.7 us
  transfers between devices with their start and end apart: 11, of which 9 were waited for; matrix products, arithmetic and copies ran while one was open for 2% of the time, Pallas kernels for 0%

commit v1 on v0

--- a/solution.py
+++ b/solution.py
@@ -1,8 +1,11 @@
+import functools
 import math
 
 import jax
 import jax.numpy as jnp
 from jax import lax
+from jax.experimental import pallas as pl
+from jax.experimental.pallas import tpu as pltpu
 from jax.sharding import PartitionSpec as P
 
 D = 1280
@@ -10,6 +13,9 @@
 DL = 4096
 KVH = 16
 LHD = 128
+MESH = pl.DeviceIdType.MESH
+F32 = jnp.float32
+BF16 = jnp.bfloat16
 
 
 def extended_2(cells, sides, width):
@@ -62,47 +68,237 @@
     return jnp.where((columns < KVH * LHD)[None, :], turned, cache)
 
 
-def attend_block(state, pairs, queries):
-    peak, weight_sum, output = state
-    heads = queries.shape[1]
-    width = heads * HD
-    length = pairs.shape[0]
-    keys_part = pairs[:, :width].reshape(length, heads, HD)
-    values_part = pairs[:, width:].reshape(length, heads, HD)
-    scores = (
-        jnp.einsum("qhd,khd->hqk", queries, keys_part, preferred_element_type=jnp.float32) * 0.125
-    )
-    fresh = jnp.maximum(peak, jnp.max(scores, axis=-1))
-    decay = jnp.exp(peak - fresh)
-    weights = jnp.exp(scores - fresh[:, :, None])
-    weight_sum = weight_sum * decay + jnp.sum(weights, axis=-1)
-    product = jnp.einsum(
-        "hqk,khd->qhd",
-        weights.astype(jnp.bfloat16),
-        values_part,
-        preferred_element_type=jnp.float32,
-    )
-    output = output * jnp.transpose(decay)[:, :, None] + product
-    return (fresh, weight_sum, output)
-
-
-def fold_keys(queries, state, piece):
-    length = piece.shape[0]
-    step_rows = math.gcd(length, 512)
-
-    def advance(index, inner):
-        pairs = lax.dynamic_slice_in_dim(piece, index * step_rows, step_rows, 0)
-        return attend_block(inner, pairs, queries)
-
-    return lax.fori_loop(0, length // step_rows, advance, state)
-
-
-def start_state(heads, count):
-    return (
-        jnp.full((heads, count), -1e30, jnp.float32),
-        jnp.zeros((heads, count), jnp.float32),
-        jnp.zeros((count, heads, HD), jnp.float32),
-    )
+def place():
+    mp, sec = lax.axis_index("mp"), lax.axis_index("section")
+    return lax.axis_index("tm"), mp // 2, mp % 2, sec // 2, sec % 2
+
+
+def device(y, x_hi, c, z, x_lo):
+    return {"tm": y, "mp": x_hi * 2 + c, "section": z * 2 + x_lo}
+
+
+def remote(src, dst, send, recv, target):
+    return pltpu.make_async_remote_copy(
+        src_ref=src, dst_ref=dst, send_sem=send, recv_sem=recv, device_id=target, device_id_type=MESH
+    )
+
+
+NEG = -1e30
+TQ = 256
+
+
+def attn_kernel(
+    pk, out, kv, qbox, qs, m, l, acc, obuf, obox,
+    kv_s, kv_r, q_s, q_r, o_s, o_r, loc, up_s, up_r, dn_s, dn_r, co_s, co_r,
+):
+    y, x_hi, c, z, x_lo = place()
+    Z = kv.shape[0]
+    n = qbox.shape[0]
+    up = device(y, x_hi, c, lax.rem(z + 1, Z), x_lo)
+    down = device(y, x_hi, c, lax.rem(z + Z - 1, Z), x_lo)
+    twin = device(y, x_hi, 1 - c, z, x_lo)
+    peers = [device(i, x_hi, x_lo, z, c) for i in range(n)]
+    mirror = c == x_lo
+
+    barrier = pltpu.get_barrier_semaphore()
+    for who in (up, down, twin):
+        pl.semaphore_signal(barrier, inc=1, device_id=who, device_id_type=MESH)
+    for i in range(n):
+        own = jnp.logical_and(mirror, y == i)
+
+        @pl.when(jnp.logical_not(own))
+        def _():
+            pl.semaphore_signal(barrier, inc=1, device_id=peers[i], device_id_type=MESH)
+
+    pl.semaphore_wait(barrier, 3 + n - mirror.astype(jnp.int32))
+
+    half = kv.shape[2] // n
+    for i in range(n):
+        own = jnp.logical_and(mirror, y == i)
+        rows = pl.ds(pl.multiple_of(y * half, half), half)
+
+        @pl.when(jnp.logical_not(own))
+        def _():
+            remote(pk.at[i, 0:half], kv.at[z, x_lo, rows], kv_s.at[i], kv_r.at[y], peers[i]).start()
+            remote(pk.at[i, half:], qbox.at[y], q_s.at[i], q_r.at[y], peers[i]).start()
+
+        @pl.when(own)
+        def _():
+            pltpu.make_async_copy(pk.at[i, 0:half], kv.at[z, c, rows], loc.at[0]).start()
+            pltpu.make_async_copy(pk.at[i, half:], qbox.at[y], loc.at[1]).start()
+
+    m[...] = jnp.full(m.shape, NEG, F32)
+    l[...] = jnp.zeros(l.shape, F32)
+    acc[...] = jnp.zeros(acc.shape, F32)
+
+    for i in range(n):
+        own = jnp.logical_and(mirror, y == i)
+        rows = pl.ds(i * half, half)
+
+        @pl.when(jnp.logical_not(own))
+        def _():
+            remote(pk.at[i, 0:half], kv.at[z, c, rows], kv_s.at[i], kv_r.at[i], peers[i]).wait()
+            remote(pk.at[i, half:], qbox.at[i], q_s.at[i], q_r.at[i], peers[i]).wait()
+
+        @pl.when(own)
+        def _():
+            pltpu.make_async_copy(pk.at[i, 0:half], kv.at[z, c, rows], loc.at[0]).wait()
+            pltpu.make_async_copy(pk.at[i, half:], qbox.at[i], loc.at[1]).wait()
+
+    def block(ref_z, core):
+        return kv.at[ref_z, core]
+
+    def send_up(t, zz):
+        return remote(block(zz, c), block(zz, c), up_s.at[t], up_r.at[t], up)
+
+    def send_down(t, zz):
+        return remote(block(zz, c), block(zz, c), dn_s.at[t], dn_r.at[t], down)
+
+    def share(k, zz):
+        return remote(block(zz, c), block(zz, c), co_s.at[k], co_r.at[k], twin)
+
+    def taken(k, zz):
+        return remote(block(zz, 1 - c), block(zz, 1 - c), co_s.at[k], co_r.at[k], twin)
+
+    send_up(0, z).start()
+    send_down(0, z).start()
+    share(0, z).start()
+
+    lanes = lax.broadcasted_iota(jnp.int32, (half // 2, 128), 1)
+    for i in range(n):
+        raw = qbox[i].astype(F32) * 0.125
+        qs[i * half : i * half + half // 2, :] = jnp.where(lanes < HD, raw, 0.0).astype(BF16)
+        qs[i * half + half // 2 : (i + 1) * half, :] = jnp.where(
+            lanes < HD, pltpu.roll(raw, HD, 1), 0.0
+        ).astype(BF16)
+
+    total = qs.shape[0]
+
+    def process(zz, core):
+        def tile(k, carry):
+            rows = pl.ds(pl.multiple_of(k * TQ, TQ), TQ)
+            pairs = kv[zz, core]
+            s = lax.dot_general(
+                qs[rows, :], pairs, (((1,), (1,)), ((), ())), preferred_element_type=F32
+            )
+            old = m[rows, :]
+            new = jnp.maximum(old, jnp.max(s, axis=1, keepdims=True))
+            m[rows, :] = new
+            decay = jnp.exp(old - new)
+            w = jnp.exp(s - new[:, 0:1])
+            l[rows, :] = l[rows, :] * decay + jnp.sum(w, axis=1, keepdims=True)
+            acc[rows, :] = acc[rows, :] * decay + jnp.dot(
+                w.astype(BF16), pairs, preferred_element_type=F32
+            )
+            return carry
+
+        lax.fori_loop(0, total // TQ, tile, 0)
+
+    process(z, c)
+    taken(0, z).wait_recv()
+    process(z, 1 - c)
+    far = Z // 2
+    for t in range(1, far + 1):
+        below = lax.rem(z + Z - t, Z)
+        above = lax.rem(z + t, Z)
+        send_up(t - 1, below).wait_recv()
+        if t < far:
+            send_up(t, below).start()
+        share(2 * t - 1, below).start()
+        if t < far:
+            send_down(t - 1, above).wait_recv()
+            if t < far - 1:
+                send_down(t, above).start()
+            share(2 * t, above).start()
+        process(below, c)
+        if t < far:
+            process(above, c)
+        taken(2 * t - 1, below).wait_recv()
+        process(below, 1 - c)
+        if t < far:
+            taken(2 * t, above).wait_recv()
+            process(above, 1 - c)
+
+    lane_q = lax.broadcasted_iota(jnp.int32, (half // 2, 128), 1)
+    for i in range(n):
+        top = pl.ds(i * half, half // 2)
+        low = pl.ds(i * half + half // 2, half // 2)
+        first = pltpu.roll(acc[top, :] / l[top, :], HD, 1)
+        second = acc[low, :] / l[low, :]
+        obuf[i] = jnp.where(lane_q < HD, first, second).astype(BF16)
+    for i in range(n):
+        own = jnp.logical_and(mirror, y == i)
+
+        @pl.when(jnp.logical_not(own))
+        def _():
+            remote(obuf.at[i], obox.at[y], o_s.at[i], o_r.at[y], peers[i]).start()
+
+        @pl.when(own)
+        def _():
+            pltpu.make_async_copy(obuf.at[i], obox.at[y], loc.at[0]).start()
+
+    for t in range(far):
+        send_up(t, z).wait_send()
+    for t in range(far - 1):
+        send_down(t, z).wait_send()
+    for k in range(2 * far):
+        share(k, z).wait_send()
+
+    for i in range(n):
+        own = jnp.logical_and(mirror, y == i)
+
+        @pl.when(jnp.logical_not(own))
+        def _():
+            remote(obuf.at[i], obox.at[i], o_s.at[i], o_r.at[i], peers[i]).wait()
+
+        @pl.when(own)
+        def _():
+            pltpu.make_async_copy(obuf.at[i], obox.at[i], loc.at[0]).wait()
+
+    for pair in range(n // 2):
+        a = obox[2 * pair].astype(F32)
+        b = obox[2 * pair + 1].astype(F32)
+        cols = slice(pair * 128, (pair + 1) * 128)
+        out[0 : half // 2, cols] = jnp.where(lane_q < HD, a, pltpu.roll(b, HD, 1)).astype(BF16)
+        out[half // 2 :, cols] = jnp.where(lane_q < HD, pltpu.roll(a, HD, 1), b).astype(BF16)
+
+
+def attention(projected, heads):
+    frames = projected.shape[0]
+    n = heads
+    Z = lax.axis_size("section") // 2
+    split = projected.reshape(frames, 3, heads, HD)
+    kvp = jnp.concatenate([split[:, 1], split[:, 2]], axis=-1).transpose(1, 0, 2)
+    q = split[:, 0].transpose(1, 0, 2)
+    qp = jnp.concatenate([q[:, : frames // 2], q[:, frames // 2 :]], axis=-1)
+    pk = jnp.concatenate([kvp, qp], axis=1)
+    total = frames * n
+    dma = pltpu.SemaphoreType.DMA
+    vm = pl.BlockSpec(memory_space=pltpu.VMEM)
+    return pl.pallas_call(
+        attn_kernel,
+        out_shape=jax.ShapeDtypeStruct((frames, heads * HD), BF16),
+        in_specs=[vm],
+        out_specs=vm,
+        scratch_shapes=[
+            pltpu.VMEM((Z, 2, total, 128), BF16),
+            pltpu.VMEM((n, frames // 2, 128), BF16),
+            pltpu.VMEM((total, 128), BF16),
+            pltpu.VMEM((total, 128), F32),
+            pltpu.VMEM((total, 128), F32),
+            pltpu.VMEM((total, 128), F32),
+            pltpu.VMEM((n, frames // 2, 128), BF16),
+            pltpu.VMEM((n, frames // 2, 128), BF16),
+            dma((n,)), dma((n,)), dma((n,)), dma((n,)), dma((n,)), dma((n,)), dma((2,)),
+            dma((Z // 2,)), dma((Z // 2,)), dma((Z // 2,)), dma((Z // 2,)), dma((Z,)), dma((Z,)),
+        ],
+        compiler_params=pltpu.CompilerParams(
+            collective_id=1, has_side_effects=True, vmem_limit_bytes=40 * 2**20
+        ),
+        cost_estimate=pl.CostEstimate(
+            flops=4 * total * total * 16 * 64, bytes_accessed=4 * 2**20, transcendentals=total * total * 16
+        ),
+    )(pk)
 
 
 def shards(
@@ -153,18 +349,7 @@
     projected = jnp.dot(piece, weight_rows, preferred_element_type=jnp.float32).astype(jnp.bfloat16)
     width = qkv_full.shape[2]
     heads = width // HD
-    queries = projected[:, :width].reshape(encoded, heads, HD)
-    pairs = projected[:, width:]
-    peak, weight_sum, output = fold_keys(
-        queries,
-        start_state(heads, encoded),
-        lax.all_gather(pairs, ("tm", "section"), axis=0, tiled=True),
-    )
-    attended = (
-        (output / jnp.transpose(weight_sum)[:, :, None])
-        .astype(jnp.bfloat16)
-        .reshape(encoded, width)
-    )
+    attended = attention(projected, heads)
     mixed = lax.psum_scatter(
         jnp.dot(attended, out_weight, preferred_element_type=jnp.float32).astype(jnp.bfloat16),
         "mp",

time: 1100 us -> 652 us (0.59)
  waiting for transfers between devices: 828 us -> 457 us
  Pallas kernels: 0 us -> 66.1 us
  local copies, waits for them, and re-layouts: 83.7 us -> 21.4 us
  matrix products: 82.1 us -> 21 us
  other arithmetic: 18.3 us -> 5.32 us
    all_gather x1 -> x0, waiting for transfers between devices: 367 us -> none  [shards(): lax.all_gather(pairs, ('tm', 'section'), axis=0, tiled=True)]
    pallas_call x0 -> x1, Pallas kernels: none -> 66.1 us  [attention(): pl.pallas_call(attn_kernel, out_shape=jax.ShapeDtypeStruct((frames, heads...]
    dot_general x64 -> x0, matrix products: 61.1 us -> none  [the longest x32 44.8 us: attend_block(): jnp.einsum('qhd,khd->hqk', queries, keys_part, preferred_element_type=jnp...]
    slice x35 -> x2, local copies, waits for them, and re-layouts: 35.5 us -> 0.05 us  [the longest x1 0.03 us: attention(): split[:, 1]]
    while x224 -> x0, local copies, waits for them, and re-layouts: 27.6 us -> none
    reduce_sum x32 -> x0, other arithmetic: 11.6 us -> none  [attend_block(): weight_sum = weight_sum * decay + jnp.sum(weights, axis=-1)]
  transfers between devices with their start and end apart: 11 -> 10, of which waited for: 9 -> 8; matrix products, arithmetic and copies ran while one was open for 2% -> 4% of each run, Pallas kernels for 0% -> 0%
where the time goes in v1:
time: 652 us
  waiting for transfers between devices  457 us (70%)
  Pallas kernels  66.1 us (10%)
  blocking collectives  57.1 us (9%)
  local copies, waits for them, and re-layouts  21.4 us (3%)
  matrix products  21 us (3%)
  between operations  13.8 us (2%)
  starting transfers between devices  10.4 us (2%)
    all_gather x1, waiting for transfers between devices, shards(): lax.all_gather(kv_weight, 'section', axis=0, tiled=True)  172 us
    all_gather x1, waiting for transfers between devices, shards(): lax.all_gather(conv2_weight, 'section', axis=1, tiled=True)  80.2 us
    pallas_call x1, Pallas kernels, attention(): pl.pallas_call(attn_kernel, out_shape=jax.ShapeDtypeStruct((frames, heads...  66.1 us
    all_gather x1, waiting for transfers between devices, shards(): lax.all_gather(qkv_weight, 'section', axis=0, tiled=True)  49.5 us
    all_gather x1, waiting for transfers between devices, shards(): lax.all_gather(proj_weight, 'section', axis=0, tiled=True)  49 us
    reduce_scatter x1, waiting for transfers between devices, shards(): lax.psum_scatter(jnp.dot(scaled, kv_full, preferred_element_type=jnp.floa...  37.8 us
    all_gather x1, waiting for transfers between devices, shards(): piece = lax.all_gather(extended, 'mp', axis=1, tiled=True)  34.7 us
    reduce_scatter x1, waiting for transfers between devices, shards(): lax.psum_scatter(jnp.dot(attended, out_weight, preferred_element_type=jnp...  29.6 us
  transfers between devices with their start and end apart: 10, of which 8 were waited for; matrix products, arithmetic and copies ran while one was open for 4% of the time, Pallas kernels for 0%

profile of v1, /device:TPU:1, one launch (start us, length us, event | category | flops | bytes accessed | tf_op | source)
XLA Modules:
  0.0 651.8 jit_solution(4723667437359015016)
XLA Ops:
  7.3 1.3 collective-permute-start.1
  8.6 4.6 collective-permute-start
  14.4 1.2 fusion.34
  15.6 2.5 fusion.5
  18.2 4.3 collective-permute-start.2
  22.5 1.5 collective-permute-done.2
  26.7 34.7 %all-gather.15.cloned.1.call-done = bf16[4,320,513]{1,2,0:T(8,128)(2,1)} async-done(((bf16[1,320,513]{1,2,0:T(8,128)(2,1)}), bf16[4,320,513]{1,2,0:T(8,128)(2,1)}) %all-gather.15.cloned.1.call-update) | async-done | bytes 1313296 | tf_op jit(solution)/shard_map/all_gather | solution.py:336
  61.4 3.2 copy.39
  64.5 3.1 reshape.73
  67.6 1.2 slice.73
  68.8 1.2 slice.75
  70.0 4.3 slice.77
  74.3 49.5 %all-gather.9.cloned.1.call-done = bf16[1280,3,256]{2,0,1:T(8,128)(2,1)} async-done(((bf16[80,3,256]{2,0,1:T(8,128)(2,1)}), bf16[1280,3,256]{2,0,1:T(8,128)(2,1)}) %all-gather.9.cloned.1.call-update) | async-done | bytes 1966096 | tf_op jit(solution)/shard_map/all_gather | solution.py:318
  123.9 4.0 copy.40
  127.9 80.2 %all-gather.7.cloned.1.call-done = bf16[3,1280,320]{2,1,0:T(8,128)(2,1)} async-done(((bf16[3,80,320]{2,1,0:T(8,128)(2,1)}), bf16[3,1280,320]{2,1,0:T(8,128)(2,1)}) %all-gather.7.cloned.1.call-update) | async-done | bytes 2457616 | tf_op jit(solution)/shard_map/all_gather | solution.py:317
  208.0 1.7 fusion.2
  209.7 1.7 convolution_add_fusion.2
  211.5 2.6 convert_reduce_fusion
  214.0 13.5 %all-reduce.1 = (f32[256]{0:T(256)S(1)}, f32[256]{0:T(256)S(1)}) all-reduce(f32[256]{0:T(256)S(1)} %get-tuple-element.8, f32[256]{0:T(256)S(1)} %get-tuple-element.7), channel_id=1, replica_groups=mesh['tm'=4,'mp'=4,'section'=16] {'mp'}, use_global_device_ids=true, to_apply=%region_3.0 | all-reduce | flops 512 | bytes 4096 | tf_op jit(solution)/shard_map/psum | solution.py:49
  227.6 10.1 %all_gather.23 = bf16[256,1280]{0,1:T(8,128)(2,1)S(1)} all-gather(bf16[256,320]{0,1:T(8,128)(2,1)S(1)} %fusion.23), channel_id=1, replica_groups=mesh['tm'=4,'mp'=4,'section'=16] {'mp'}, dimensions={1}, use_global_device_ids=true | all-gather | bytes 819200 | tf_op jit(solution)/shard_map/all_gather | solution.py:347
  239.5 66.1 %shard_map.100 = bf16[256,256]{1,0:T(8,128)(2,1)S(1)} custom-call(bf16[4,384,128]{2,1,0:T(8,128)(2,1)S(1)} %maximum_maximum_fusion.pk), custom_call_target="tpu_custom_call" | custom-call | flops 4294967296 | bytes 4194304 | tf_op jit(solution)/shard_map/pallas_call | solution.py:278
  305.7 1.2 convolution_convert_fusion.1
  308.1 29.6 %reduce-scatter.3.cloned.1.call-done = bf16[256,320]{0,1:T(8,128)(2,1)} async-done(((bf16[256,1280]{0,1:T(8,128)(2,1)}), bf16[256,320]{0,1:T(8,128)(2,1)}) %reduce-scatter.3.cloned.1.call-update) | async-done | bytes 163856 | tf_op jit(solution)/shard_map/reduce_scatter | solution.py:353
  339.7 7.4 %all-reduce = (f32[128]{0:T(128)S(1)}, f32[128]{0:T(128)S(1)}) all-reduce(f32[128]{0:T(128)S(1)} %get-tuple-element.6, f32[128]{0:T(128)S(1)} %get-tuple-element.5), channel_id=1, replica_groups=mesh['tm'=4,'mp'=4,'section'=16] {'mp'}, use_global_device_ids=true, to_apply=%region_9.0 | all-reduce | flops 256 | bytes 2048 | tf_op jit(solution)/shard_map/psum | solution.py:49
  347.3 11.2 %all_gather.25 = bf16[128,1280]{0,1:T(8,128)(2,1)S(1)} all-gather(bf16[128,320]{0,1:T(8,128)(2,1)S(1)} %copy.46), channel_id=1, replica_groups=mesh['tm'=4,'mp'=4,'section'=16] {'mp'}, dimensions={1}, use_global_device_ids=true | all-gather | bytes 409600 | tf_op jit(solution)/shard_map/all_gather | solution.py:365
  358.6 49.0 %all-gather.11.cloned.1.call-done = bf16[1280,1024]{1,0:T(8,128)(2,1)} async-done(((bf16[80,1024]{1,0:T(8,128)(2,1)}), bf16[1280,1024]{1,0:T(8,128)(2,1)}) %all-gather.11.cloned.1.call-update) | async-done | bytes 2621456 | tf_op jit(solution)/shard_map/all_gather | solution.py:319
  407.5 2.4 multiply_reduce_fusion
  409.9 14.9 %psum.39 = f32[128]{0:T(128)S(1)} all-reduce(f32[128]{0:T(128)S(1)} %get-tuple-element.27), channel_id=1, replica_groups=mesh['tm'=4,'mp'=4,'section'=16] {'mp'}, use_global_device_ids=true, to_apply=%region_11.0 | all-reduce | flops 128 | bytes 1024 | tf_op jit(solution)/shard_map/psum | solution.py:370
  424.8 172.1 %all-gather.13.cloned.1.call-done = bf16[1024,4096]{1,0:T(8,128)(2,1)} async-done(((bf16[64,4096]{1,0:T(8,128)(2,1)}), bf16[1024,4096]{1,0:T(8,128)(2,1)}) %all-gather.13.cloned.1.call-update) | async-done | bytes 8388624 | tf_op jit(solution)/shard_map/all_gather | solution.py:320
  596.9 5.7 convolution_convert_fusion
  602.7 37.8 %reduce-scatter.5.cloned.1.call-done = bf16[128,1024]{1,0:T(8,128)(2,1)} async-done(((bf16[128,4096]{1,0:T(8,128)(2,1)}), bf16[128,1024]{1,0:T(8,128)(2,1)}) %reduce-scatter.5.cloned.1.call-update) | async-done | bytes 262160 | tf_op jit(solution)/shard_map/reduce_scatter | solution.py:372
  642.0 3.0 fusion.16
  (62 shorter events, 11.4 us)
Async XLA Ops:
  6.5 299.1 %copy-start = (bf16[256,1280]{1,0:T(8,128)(2,1)S(1)}, bf16[256,1280]{1,0:T(8,128)(2,1)}, u32[]{:S(2)}) copy-start(bf16[256,1280]{1,0:T(8,128)(2,1)} %param.15) | copy-start | bytes 1966084
  6.5 54.8 %all-gather.15.cloned.1.call-start = ((), (), s32[]{:S(2)}) async-start(), calls=%async_computation.8 | async-start | bytes 1996800 | tf_op jit(solution)/shard_map/all_gather | solution.py:336
  7.3 7.1 %collective-permute-start.1 = (bf16[1,128]{1,0:T(2,128)(2,1)S(1)}, bf16[1,128]{1,0:T(2,128)(2,1)S(1)}, u32[]{:S(2)}, u32[]{:S(2)}) collective-permute-start(bf16[1,128]{1,0:T(2,128)(2,1)S(1)} %get-tuple-element.21), channel_id=1, source_target_pairs={{1,0},{2,1},{3,2},{4,3},{5,4},{6,5},{7,6},{8,7},{9,8},{10,9},{11,1... | collective-permute-start | bytes 776 | tf_op jit(solution)/shard_map/ppermute | solution.py:31
  8.6 7.0 %collective-permute-start = (bf16[1,128]{1,0:T(2,128)(2,1)S(1)}, bf16[1,128]{1,0:T(2,128)(2,1)S(1)}, u32[]{:S(2)}, u32[]{:S(2)}) collective-permute-start(bf16[1,128]{1,0:T(2,128)(2,1)S(1)} %get-tuple-element.20), channel_id=1, source_target_pairs={{0,1},{1,2},{2,3},{3,4},{4,5},{5,6},{6,7},{7,8},{8,9},{9,10},{10,1... | collective-permute-start | bytes 776 | tf_op jit(solution)/shard_map/ppermute | solution.py:29
  18.2 5.7 collective-permute-start.2
  25.1 98.8 %all-gather.9.cloned.1.call-start = ((), (), s32[]{:S(2)}) async-start(), calls=%async_computation.3 | async-start | bytes 2088960 | tf_op jit(solution)/shard_map/all_gather | solution.py:318
  25.9 182.1 %all-gather.7.cloned.1.call-start = ((), (), s32[]{:S(2)}) async-start(), calls=%async_computation.2 | async-start | bytes 3133440 | tf_op jit(solution)/shard_map/all_gather | solution.py:317
  26.6 311.1 %reduce-scatter.3.cloned.1.call-start = ((), (), s32[]{:S(2)}) async-start(), calls=%async_computation.4 | async-start | bytes 819200 | tf_op jit(solution)/shard_map/reduce_scatter | solution.py:353
  127.9 83.6 %copy-start.3 = (bf16[256,1280]{1,0:T(8,128)(2,1)S(1)}, bf16[256,1280]{1,0:T(8,128)(2,1)}, u32[]{:S(2)}) copy-start(bf16[256,1280]{1,0:T(8,128)(2,1)} %slice.77) | copy-start | bytes 1966084
  211.5 16.0 %copy-start.6 = (f32[320]{0:T(512)S(1)}, f32[320]{0:T(512)}, u32[]{:S(2)}) copy-start(f32[320]{0:T(512)} %param.13) | copy-start | bytes 3844
  211.5 26.3 %copy-start.1 = (bf16[1280,3,256]{0,2,1:T(8,128)(2,1)S(1)}, bf16[1280,3,256]{0,2,1:T(8,128)(2,1)}, u32[]{:S(2)}) copy-start(bf16[1280,3,256]{0,2,1:T(8,128)(2,1)} %copy.40) | copy-start | bytes 5898244
  305.6 41.4 %copy-start.5 = (f32[320]{0:T(512)S(1)}, f32[320]{0:T(512)}, u32[]{:S(2)}) copy-start(f32[320]{0:T(512)} %param.16) | copy-start | bytes 3844
  306.9 100.6 %all-gather.11.cloned.1.call-start = ((), (), s32[]{:S(2)}) async-start(), calls=%async_computation.5 | async-start | bytes 2785280 | tf_op jit(solution)/shard_map/all_gather | solution.py:319
  307.5 289.4 %all-gather.13.cloned.1.call-start = ((), (), s32[]{:S(2)}) async-start(), calls=%async_computation.6 | async-start | bytes 8912896 | tf_op jit(solution)/shard_map/all_gather | solution.py:320
  308.1 332.4 %reduce-scatter.5.cloned.1.call-start = ((), (), s32[]{:S(2)}) async-start(), calls=%async_computation.7 | async-start | bytes 1310720 | tf_op jit(solution)/shard_map/reduce_scatter | solution.py:372
  339.1 257.8 %copy-start.4 = (f32[1024]{0:T(1024)S(1)}, f32[1024]{0:T(1024)}, u32[]{:S(2)}) copy-start(f32[1024]{0:T(1024)} %param.18) | copy-start | bytes 12292
  640.5 1.5 copy-start.2
Sparse Core Ops, SparseCore 0:
  25.2 36.0 all-gather.14
  63.2 60.6 all-gather.8
  125.7 82.3 all-gather.6
  307.0 30.6 reduce-scatter.2
  339.4 68.0 all-gather.10
  409.2 187.6 all-gather.12
  602.8 37.6 reduce-scatter.4

commit v2 on v1

--- a/solution.py
+++ b/solution.py
@@ -85,32 +85,283 @@
 
 NEG = -1e30
 TQ = 256
-
-
-def attn_kernel(
-    pk, out, kv, qbox, qs, m, l, acc, obuf, obox,
-    kv_s, kv_r, q_s, q_r, o_s, o_r, loc, up_s, up_r, dn_s, dn_r, co_s, co_r,
+H0 = 32
+
+
+def greet(Z, Y):
+    y, x_hi, c, z, x_lo = place()
+    barrier = pltpu.get_barrier_semaphore()
+    for step in (1, Z - 1):
+        pl.semaphore_signal(
+            barrier, inc=1, device_id=device(y, x_hi, c, lax.rem(z + step, Z), x_lo), device_id_type=MESH
+        )
+    for dy in range(Y):
+        for k in range(8):
+            if dy == 0 and k == 0:
+                continue
+            a, b, d = k // 4, (k // 2) % 2, k % 2
+            other = device(
+                lax.rem(y + dy, Y), lax.rem(x_hi + a, 2), lax.rem(c + b, 2), z, lax.rem(x_lo + d, 2)
+            )
+            pl.semaphore_signal(barrier, inc=1, device_id=other, device_id_type=MESH)
+    pl.semaphore_wait(barrier, 8 * Y + 1)
+
+
+class Across:
+    def __init__(self, src, buf, send, recv):
+        y, x_hi, c, z, x_lo = place()
+        self.buf, self.send, self.recv, self.src = buf, send, recv, src
+        self.me, self.twin, self.far, self.both = (
+            x_hi * 2 + c, x_hi * 2 + 1 - c, (1 - x_hi) * 2 + c, (1 - x_hi) * 2 + 1 - c
+        )
+        self.to_twin = device(y, x_hi, 1 - c, z, x_lo)
+        self.to_far = device(y, 1 - x_hi, c, z, x_lo)
+
+    def copy(self, k, src, slot, target):
+        return remote(src, self.buf.at[slot], self.send.at[k], self.recv.at[k], target)
+
+    def start(self):
+        self.copy(1, self.src, self.me, self.to_far).start()
+        self.copy(0, self.src, self.me, self.to_twin).start()
+
+    def relay(self):
+        self.copy(1, self.buf.at[self.far], self.far, self.to_far).wait_recv()
+        self.copy(2, self.buf.at[self.far], self.far, self.to_twin).start()
+
+    def finish(self):
+        self.copy(0, self.buf.at[self.twin], self.twin, self.to_twin).wait_recv()
+        self.copy(2, self.buf.at[self.both], self.both, self.to_twin).wait_recv()
+        for k in range(3):
+            self.copy(k, self.buf.at[self.me], self.me, self.to_twin).wait_send()
+
+
+class Sections:
+    def __init__(self, src, buf, us, ur, ds, dr, ous, our, ods, odr, xs, xr, loc, h0):
+        y, x_hi, c, z, x_lo = place()
+        self.Z = buf.shape[0]
+        self.src, self.buf, self.z, self.x = src, buf, z, x_lo
+        self.s = (us, ur, ds, dr, ous, our, ods, odr, xs, xr)
+        self.loc = loc
+        self.lo = pl.ds(0, h0)
+        self.hi = pl.ds(h0, src.shape[0] - h0)
+        self.up = device(y, x_hi, c, lax.rem(z + 1, self.Z), x_lo)
+        self.down = device(y, x_hi, c, lax.rem(z + self.Z - 1, self.Z), x_lo)
+        self.side = device(y, x_hi, c, z, 1 - x_lo)
+
+    def below(self, t):
+        return lax.rem(self.z + self.Z - t, self.Z)
+
+    def above(self, t):
+        return lax.rem(self.z + t, self.Z)
+
+    def ring(self, kind, t, zz, src=None):
+        us, ur, ds, dr, ous, our, ods, odr, xs, xr = self.s
+        if kind == "u":
+            ref = self.buf.at[zz, self.x]
+            return remote(ref if src is None else src, ref, us.at[t], ur.at[t], self.up)
+        if kind == "d":
+            ref = self.buf.at[zz, self.x]
+            return remote(ref if src is None else src, ref, ds.at[t], dr.at[t], self.down)
+        ref = self.buf.at[zz, 1 - self.x, self.lo]
+        if kind == "ou":
+            return remote(ref, ref, ous.at[t], our.at[t], self.up)
+        return remote(ref, ref, ods.at[t], odr.at[t], self.down)
+
+    def whole(self, x):
+        us, ur, ds, dr, ous, our, ods, odr, xs, xr = self.s
+        return remote(self.src, self.buf.at[self.z, x], xs.at[0], xr.at[0], self.side)
+
+    def forward(self, k, zz, x):
+        us, ur, ds, dr, ous, our, ods, odr, xs, xr = self.s
+        ref = self.buf.at[zz, x, self.hi]
+        return remote(ref, ref, xs.at[k], xr.at[k], self.side)
+
+    def local(self):
+        return pltpu.make_async_copy(self.src, self.buf.at[self.z, self.x], self.loc)
+
+    def start(self):
+        self.local().start()
+        self.whole(self.x).start()
+        self.ring("u", 0, self.z, self.src).start()
+        self.ring("d", 0, self.z, self.src).start()
+
+    def start_other(self):
+        self.whole(1 - self.x).wait_recv()
+        self.ring("ou", 0, self.z).start()
+        self.ring("od", 0, self.z).start()
+
+    def step(self, t):
+        far = self.Z // 2
+        zz = self.below(t)
+        self.ring("u", t - 1, zz).wait_recv()
+        if t < far:
+            self.ring("u", t, zz).start()
+        self.forward(2 * t - 1, zz, self.x).start()
+        if t < far:
+            zz = self.above(t)
+            self.ring("d", t - 1, zz).wait_recv()
+            if t < far - 1:
+                self.ring("d", t, zz).start()
+            self.forward(2 * t, zz, self.x).start()
+        self.step_other(t)
+
+    def step_other(self, t):
+        far = self.Z // 2
+        zz = self.below(t)
+        self.ring("ou", t - 1, zz).wait_recv()
+        if t < far:
+            self.ring("ou", t, zz).start()
+            zz = self.above(t)
+            self.ring("od", t - 1, zz).wait_recv()
+            if t < far - 1:
+                self.ring("od", t, zz).start()
+
+    def finish(self):
+        far = self.Z // 2
+        for t in range(1, far + 1):
+            self.forward(2 * t - 1, self.below(t), 1 - self.x).wait_recv()
+            if t < far:
+                self.forward(2 * t, self.above(t), 1 - self.x).wait_recv()
+        self.local().wait()
+        self.whole(self.x).wait_send()
+        for t in range(far):
+            self.ring("u", t, self.z).wait_send()
+            self.ring("ou", t, self.z).wait_send()
+        for t in range(far - 1):
+            self.ring("d", t, self.z).wait_send()
+            self.ring("od", t, self.z).wait_send()
+        for k in range(1, 2 * far):
+            self.forward(k, self.z, self.x).wait_send()
+
+
+class Quarters:
+    def __init__(self, src, buf, us, ur, ds, dr, xs, xr, yus, yur, yds, ydr, rus, rur, rds, rdr, loc):
+        y, x_hi, c, z, x_lo = place()
+        self.Z, self.Y = buf.shape[0], buf.shape[2]
+        self.src, self.buf, self.z, self.x, self.y = src, buf, z, x_lo, y
+        self.s = (us, ur, ds, dr, xs, xr, yus, yur, yds, ydr, rus, rur, rds, rdr)
+        self.loc = loc
+        self.up = device(y, x_hi, c, lax.rem(z + 1, self.Z), x_lo)
+        self.down = device(y, x_hi, c, lax.rem(z + self.Z - 1, self.Z), x_lo)
+        self.side = device(y, x_hi, c, z, 1 - x_lo)
+        self.yn, self.yp = lax.rem(y + 1, self.Y), lax.rem(y + self.Y - 1, self.Y)
+        self.yf = lax.rem(y + 2, self.Y)
+        self.next = device(self.yn, x_hi, c, z, x_lo)
+        self.prev = device(self.yp, x_hi, c, z, x_lo)
+
+    def zs(self, k):
+        if k % 2:
+            return lax.rem(self.z + self.Z - (k + 1) // 2, self.Z)
+        return lax.rem(self.z + k // 2, self.Z)
+
+    def ring(self, kind, t, zz):
+        us, ur, ds, dr = self.s[:4]
+        ref = self.buf.at[zz, :, self.y]
+        if kind == "u":
+            return remote(ref, ref, us.at[t], ur.at[t], self.up)
+        return remote(ref, ref, ds.at[t], dr.at[t], self.down)
+
+    def cross(self, x):
+        xs, xr = self.s[4:6]
+        return remote(self.src.at[self.y], self.buf.at[self.z, x, self.y], xs.at[0], xr.at[0], self.side)
+
+    def local(self):
+        return pltpu.make_async_copy(self.src, self.buf.at[self.z, self.x], self.loc)
+
+    def spread(self, kind, k, quarter):
+        yus, yur, yds, ydr = self.s[6:10]
+        if k == 0:
+            ref = self.buf.at[self.z, 1 - self.x, quarter]
+        else:
+            ref = self.buf.at[self.zs(k), :, quarter]
+        if kind == "n":
+            return remote(ref, ref, yus.at[k], yur.at[k], self.next)
+        return remote(ref, ref, yds.at[k], ydr.at[k], self.prev)
+
+    def relay(self, kind, k, quarter):
+        rus, rur, rds, rdr = self.s[10:14]
+        if kind == "n":
+            ref = self.buf.at[self.zs(k), (1 - self.x) if k == 0 else 0, quarter]
+            return remote(ref, ref, rus.at[k], rur.at[k], self.next)
+        ref = self.buf.at[self.zs(k), 1, quarter]
+        return remote(ref, ref, rds.at[k], rdr.at[k], self.prev)
+
+    def start(self):
+        self.cross(self.x).start()
+        self.local().start()
+
+    def begin(self):
+        self.local().wait()
+        self.cross(1 - self.x).wait_recv()
+        self.spread("n", 0, self.y).start()
+        self.spread("p", 0, self.y).start()
+        self.ring("u", 0, self.z).start()
+        self.ring("d", 0, self.z).start()
+
+    def arrive(self, k):
+        far, t, zz = self.Z // 2, (k + 1) // 2, self.zs(k)
+        kind = "u" if k % 2 else "d"
+        self.ring(kind, t - 1, zz).wait_recv()
+        if t < (far if kind == "u" else far - 1):
+            self.ring(kind, t, zz).start()
+        self.spread("n", k, self.y).start()
+        self.spread("p", k, self.y).start()
+
+    def pass_on(self, k):
+        self.spread("n", k, self.yp).wait_recv()
+        self.relay("n", k, self.yp).start()
+        self.spread("p", k, self.yn).wait_recv()
+        if k:
+            self.relay("p", k, self.yn).start()
+
+    def finish(self):
+        far = self.Z // 2
+        for k in range(2 * far):
+            self.relay("n", k, self.yf).wait_recv()
+            if k:
+                self.relay("p", k, self.yf).wait_recv()
+        self.cross(self.x).wait_send()
+        for t in range(far):
+            self.ring("u", t, self.z).wait_send()
+        for t in range(far - 1):
+            self.ring("d", t, self.z).wait_send()
+        for k in range(2 * far):
+            self.spread("n", k, self.y).wait_send()
+            self.spread("p", k, self.y).wait_send()
+            self.relay("n", k, self.y).wait_send()
+            if k:
+                self.relay("p", k, self.y).wait_send()
+
+
+def normal(rows, gain):
+    center = jnp.mean(rows, axis=-1, keepdims=True)
+    spread = jnp.mean(jnp.square(rows - center), axis=-1, keepdims=True)
+    return (rows - center) * lax.rsqrt(spread + 1e-05) * gain
+
+
+def tail_kernel(
+    pk, hq, ow, pw, kw, pg, rg, cs, sn, out,
+    kv, qbox, qs, m, l, acc, obuf, abox, att, res, owf, pwf, kwf, pbox, sbox, keep, tsend, trecv, csend, crecv,
+    kv_s, kv_r, q_s, q_r, loc, up_s, up_r, dn_s, dn_r, co_s, co_r, a_s, a_r,
+    ow_s, ow_r, pb_s, pb_r, sb_s, sb_r, t_s, t_r, c_s, c_r,
+    p0, p1, p2, p3, p4, p5, p6, p7, p8, p9,
+    k0, k1, k2, k3, k4, k5, k6, k7, k8, k9, k10, k11, k12, k13,
 ):
     y, x_hi, c, z, x_lo = place()
     Z = kv.shape[0]
     n = qbox.shape[0]
+    me = x_hi * 2 + c
     up = device(y, x_hi, c, lax.rem(z + 1, Z), x_lo)
     down = device(y, x_hi, c, lax.rem(z + Z - 1, Z), x_lo)
     twin = device(y, x_hi, 1 - c, z, x_lo)
+    far_dev = device(y, 1 - x_hi, c, z, x_lo)
     peers = [device(i, x_hi, x_lo, z, c) for i in range(n)]
     mirror = c == x_lo
-
-    barrier = pltpu.get_barrier_semaphore()
-    for who in (up, down, twin):
-        pl.semaphore_signal(barrier, inc=1, device_id=who, device_id_type=MESH)
-    for i in range(n):
-        own = jnp.logical_and(mirror, y == i)
-
-        @pl.when(jnp.logical_not(own))
-        def _():
-            pl.semaphore_signal(barrier, inc=1, device_id=peers[i], device_id_type=MESH)
-
-    pl.semaphore_wait(barrier, 3 + n - mirror.astype(jnp.int32))
+    greet(Z, n)
+
+    outw = Across(ow, owf, ow_s, ow_r)
+    proj = Sections(pw, pwf, p0, p1, p2, p3, p4, p5, p6, p7, p8, p9, loc.at[3], H0)
+    kvw = Quarters(kw, kwf, k0, k1, k2, k3, k4, k5, k6, k7, k8, k9, k10, k11, k12, k13, loc.at[4])
 
     half = kv.shape[2] // n
     for i in range(n):
@@ -127,6 +378,10 @@
             pltpu.make_async_copy(pk.at[i, 0:half], kv.at[z, c, rows], loc.at[0]).start()
             pltpu.make_async_copy(pk.at[i, half:], qbox.at[y], loc.at[1]).start()
 
+    kvw.start()
+    own_w = pltpu.make_async_copy(ow, owf.at[me], loc.at[5])
+    own_w.start()
+
     m[...] = jnp.full(m.shape, NEG, F32)
     l[...] = jnp.zeros(l.shape, F32)
     acc[...] = jnp.zeros(acc.shape, F32)
@@ -163,6 +418,7 @@
     send_up(0, z).start()
     send_down(0, z).start()
     share(0, z).start()
+    outw.start()
 
     lanes = lax.broadcasted_iota(jnp.int32, (half // 2, 128), 1)
     for i in range(n):
@@ -173,6 +429,7 @@
         ).astype(BF16)
 
     total = qs.shape[0]
+    width = kv.shape[2]
 
     def process(zz, core):
         def tile(k, carry):
@@ -185,8 +442,11 @@
             new = jnp.maximum(old, jnp.max(s, axis=1, keepdims=True))
             m[rows, :] = new
             decay = jnp.exp(old - new)
-            w = jnp.exp(s - new[:, 0:1])
-            l[rows, :] = l[rows, :] * decay + jnp.sum(w, axis=1, keepdims=True)
+            w = jnp.exp(s - jnp.concatenate([new] * (width // 128), axis=1))
+            part = w[:, 0:128]
+            for piece in range(1, width // 128):
+                part = part + w[:, piece * 128 : (piece + 1) * 128]
+            l[rows, :] = l[rows, :] * decay + part
             acc[rows, :] = acc[rows, :] * decay + jnp.dot(
                 w.astype(BF16), pairs, preferred_element_type=F32
             )
@@ -194,10 +454,12 @@
 
         lax.fori_loop(0, total // TQ, tile, 0)
 
+    kvw.begin()
     process(z, c)
     taken(0, z).wait_recv()
     process(z, 1 - c)
     far = Z // 2
+    kvw.pass_on(0)
     for t in range(1, far + 1):
         below = lax.rem(z + Z - t, Z)
         above = lax.rem(z + t, Z)
@@ -211,31 +473,61 @@
                 send_down(t, above).start()
             share(2 * t, above).start()
         process(below, c)
+        kvw.arrive(2 * t - 1)
+        if t < far:
+            kvw.arrive(2 * t)
+        if t > 1:
+            kvw.pass_on(2 * t - 3)
+            kvw.pass_on(2 * t - 2)
         if t < far:
             process(above, c)
+        if t == 1:
+            proj.start()
         taken(2 * t - 1, below).wait_recv()
         process(below, 1 - c)
+        if t == 2:
+            proj.start_other()
+            outw.relay()
+        if t == 3:
+            proj.step(1)
         if t < far:
             taken(2 * t, above).wait_recv()
             process(above, 1 - c)
-
-    lane_q = lax.broadcasted_iota(jnp.int32, (half // 2, 128), 1)
-    for i in range(n):
-        top = pl.ds(i * half, half // 2)
-        low = pl.ds(i * half + half // 2, half // 2)
-        first = pltpu.roll(acc[top, :] / l[top, :], HD, 1)
-        second = acc[low, :] / l[low, :]
-        obuf[i] = jnp.where(lane_q < HD, first, second).astype(BF16)
-    for i in range(n):
-        own = jnp.logical_and(mirror, y == i)
-
-        @pl.when(jnp.logical_not(own))
-        def _():
-            remote(obuf.at[i], obox.at[y], o_s.at[i], o_r.at[y], peers[i]).start()
-
-        @pl.when(own)
-        def _():
-            pltpu.make_async_copy(obuf.at[i], obox.at[y], loc.at[0]).start()
+        if t == 3:
+            proj.step(2)
+        if t == 4:
+            proj.step(3)
+
+    quarter = half // 4
+    low = lax.broadcasted_iota(jnp.int32, (quarter // 2, 128), 1) < HD
+    head = (x_hi * 2 + x_lo) * n + y
+
+    def give(j, q, slot, sem):
+        k = 4 * j + q
+        return remote(obuf.at[k], abox.at[slot], a_s.at[k], a_r.at[sem], device(j, q // 2, q % 2, z, c))
+
+    for j in range(n):
+        for q in range(4):
+            k = 4 * j + q
+            at = j * half + q * quarter
+            top, bot = pl.ds(at, quarter // 2), pl.ds(at + quarter // 2, quarter // 2)
+            first = pltpu.roll(acc[top, :] / jnp.sum(l[top, :], axis=1, keepdims=True), HD, 1)
+            second = acc[bot, :] / jnp.sum(l[bot, :], axis=1, keepdims=True)
+            obuf[k] = jnp.where(low, first, second).astype(BF16)
+    for j in range(n):
+        for q in range(4):
+            own = jnp.logical_and(mirror, jnp.logical_and(y == j, me == q))
+
+            @pl.when(jnp.logical_not(own))
+            def _():
+                give(j, q, head, head).start()
+
+            @pl.when(own)
+            def _():
+                pltpu.make_async_copy(obuf.at[4 * j + q], abox.at[head], loc.at[0]).start()
+
+    proj.step(far)
+    kvw.pass_on(2 * far - 1)
 
     for t in range(far):
         send_up(t, z).wait_send()
@@ -243,62 +535,170 @@
         send_down(t, z).wait_send()
     for k in range(2 * far):
         share(k, z).wait_send()
-
-    for i in range(n):
-        own = jnp.logical_and(mirror, y == i)
+    outw.finish()
+    own_w.wait()
+
+    for h in range(4 * n):
+        own = jnp.logical_and(mirror, head == h)
 
         @pl.when(jnp.logical_not(own))
         def _():
-            remote(obuf.at[i], obox.at[i], o_s.at[i], o_r.at[i], peers[i]).wait()
+            remote(obuf.at[h], abox.at[h], a_s.at[h], a_r.at[h], twin).wait_recv()
 
         @pl.when(own)
         def _():
-            pltpu.make_async_copy(obuf.at[i], obox.at[i], loc.at[0]).wait()
-
-    for pair in range(n // 2):
-        a = obox[2 * pair].astype(F32)
-        b = obox[2 * pair + 1].astype(F32)
+            pltpu.make_async_copy(obuf.at[h], abox.at[h], loc.at[0]).wait()
+
+    for pair in range(2 * n):
+        a = abox[2 * pair].astype(F32)
+        b = abox[2 * pair + 1].astype(F32)
         cols = slice(pair * 128, (pair + 1) * 128)
-        out[0 : half // 2, cols] = jnp.where(lane_q < HD, a, pltpu.roll(b, HD, 1)).astype(BF16)
-        out[half // 2 :, cols] = jnp.where(lane_q < HD, pltpu.roll(a, HD, 1), b).astype(BF16)
-
-
-def attention(projected, heads):
+        att[0 : quarter // 2, cols] = jnp.where(low, a, pltpu.roll(b, HD, 1)).astype(BF16)
+        att[quarter // 2 :, cols] = jnp.where(low, pltpu.roll(a, HD, 1), b).astype(BF16)
+
+    mixed = jnp.dot(
+        att[...], owf[...].reshape(4 * ow.shape[0], ow.shape[1]), preferred_element_type=F32
+    )
+    tokens = quarter // 2
+    pieces = []
+    for k in range(hq.shape[1] // 128):
+        at = slice(k * 128, (k + 1) * 128)
+        res[k] = hq[:, at].astype(F32) + mixed[:, at]
+        pieces.append(
+            (res.at[k][pl.ds(0, tokens, stride=2), :] + res.at[k][pl.ds(1, tokens, stride=2), :]) * 0.5
+        )
+    pooled = jnp.concatenate(pieces, axis=1)
+    pbox[me] = normal(pooled, pg[0:1, :]).astype(BF16)
+    gather = Across(pbox.at[me], pbox, pb_s, pb_r)
+    gather.start()
+    gather.relay()
+    proj.finish()
+    gather.finish()
+
+    post = pbox[...].reshape(4 * tokens, pbox.shape[2])
+    embedded = jnp.dot(
+        post, pwf[...].reshape(2 * Z * pw.shape[0], pw.shape[1]), preferred_element_type=F32
+    ).astype(BF16)
+    widened = embedded.astype(F32)
+    sbox[me] = jnp.broadcast_to(
+        jnp.sum(widened * widened, axis=1, keepdims=True), (4 * tokens, 128)
+    )
+    squares = Across(sbox.at[me], sbox, sb_s, sb_r)
+    squares.start()
+    gained = (widened * rg[0:1, :]).astype(BF16)
+    cols = pw.shape[1]
+    kvw.finish()
+
+    def columns(a, b):
+        at = pl.ds(pl.multiple_of((a * 2 + b) * cols, cols), cols)
+        return jnp.dot(
+            gained, kwf[:, :, :, :, at].reshape(cols, cols), preferred_element_type=F32
+        )
+
+    def swap(k):
+        return remote(tsend.at[k], trecv.at[k], t_s.at[k], t_r.at[k], twin)
+
+    over = remote(csend, crecv, c_s.at[0], c_r.at[0], far_dev)
+    tsend[0] = columns(1 - x_hi, 1 - c).astype(BF16)
+    swap(0).start()
+    keep[...] = columns(1 - x_hi, c)
+    squares.relay()
+    swap(0).wait_recv()
+    csend[...] = (keep[...] + trecv[0].astype(F32)).astype(BF16)
+    over.start()
+    tsend[1] = columns(x_hi, 1 - c).astype(BF16)
+    swap(1).start()
+    keep[...] = columns(x_hi, c)
+    squares.finish()
+    scale = lax.rsqrt((sbox[0] + sbox[1] + sbox[2] + sbox[3]) / DL + 1e-06)
+    swap(1).wait_recv()
+    keep[...] = keep[...] + trecv[1].astype(F32)
+    over.wait_recv()
+    for h in range(cols // LHD):
+        at = slice(h * LHD, (h + 1) * LHD)
+        value = (keep[:, at] + crecv[:, at].astype(F32)) * scale
+        out[:, at] = (value * cs[...] + pltpu.roll(value, HD, 1) * sn[...]).astype(BF16)
+
+    swap(0).wait_send()
+    swap(1).wait_send()
+    over.wait_send()
+    for j in range(n):
+        for q in range(4):
+            own = jnp.logical_and(mirror, jnp.logical_and(y == j, me == q))
+
+            @pl.when(jnp.logical_not(own))
+            def _():
+                give(j, q, head, head).wait_send()
+
+
+def tail(pk, hq, ow, pw, kw, pg, rg, cs, sn):
+    n = pk.shape[0]
+    frames = pk.shape[1] * 2 // 3
+    Z = lax.axis_size("section") // 2
+    total = frames * n
+    tokens = frames // 2
+    quarter = frames // 4
+    cols = pw.shape[1]
+    sem = pltpu.SemaphoreType.DMA
+    vm = pl.BlockSpec(memory_space=pltpu.VMEM)
+    V = pltpu.VMEM
+    half = Z // 2
+    return pl.pallas_call(
+        tail_kernel,
+        out_shape=jax.ShapeDtypeStruct((tokens, cols), BF16),
+        in_specs=[vm] * 9,
+        out_specs=vm,
+        scratch_shapes=[
+            V((Z, 2, total, 128), BF16),
+            V((n, tokens, 128), BF16),
+            V((total, 128), BF16),
+            V((total, 128), F32),
+            V((total, 128), F32),
+            V((total, 128), F32),
+            V((16, quarter // 2, 128), BF16),
+            V((16, quarter // 2, 128), BF16),
+            V((quarter, ow.shape[0] * 4), BF16),
+            V((ow.shape[1] // 128, quarter, 128), F32),
+            V((4,) + ow.shape, BF16),
+            V((Z, 2) + pw.shape, BF16),
+            V((Z, 2) + kw.shape, BF16),
+            V((4, quarter // 2, ow.shape[1]), BF16),
+            V((4, tokens, 128), F32),
+            V((tokens, cols), F32),
+            V((2, tokens, cols), BF16),
+            V((2, tokens, cols), BF16),
+            V((tokens, cols), BF16),
+            V((tokens, cols), BF16),
+            sem((n,)), sem((n,)), sem((n,)), sem((n,)), sem((6,)),
+            sem((half,)), sem((half,)), sem((half,)), sem((half,)), sem((Z,)), sem((Z,)), sem((16,)), sem((16,)),
+            sem((3,)), sem((3,)), sem((3,)), sem((3,)), sem((3,)), sem((3,)), sem((2,)), sem((2,)), sem((1,)), sem((1,)),
+        ]
+        + [sem((half,))] * 8 + [sem((Z,))] * 2
+        + [sem((half,))] * 4 + [sem((1,))] * 2 + [sem((Z,))] * 8,
+        compiler_params=pltpu.CompilerParams(
+            collective_id=1, has_side_effects=True, vmem_limit_bytes=56 * 2**20
+        ),
+    )(pk, hq, ow, pw, kw, pg, rg, cs, sn)
+
+
+def pack(projected, heads):
     frames = projected.shape[0]
-    n = heads
-    Z = lax.axis_size("section") // 2
     split = projected.reshape(frames, 3, heads, HD)
     kvp = jnp.concatenate([split[:, 1], split[:, 2]], axis=-1).transpose(1, 0, 2)
     q = split[:, 0].transpose(1, 0, 2)
     qp = jnp.concatenate([q[:, : frames // 2], q[:, frames // 2 :]], axis=-1)
-    pk = jnp.concatenate([kvp, qp], axis=1)
-    total = frames * n
-    dma = pltpu.SemaphoreType.DMA
-    vm = pl.BlockSpec(memory_space=pltpu.VMEM)
-    return pl.pallas_call(
-        attn_kernel,
-        out_shape=jax.ShapeDtypeStruct((frames, heads * HD), BF16),
-        in_specs=[vm],
-        out_specs=vm,
-        scratch_shapes=[
-            pltpu.VMEM((Z, 2, total, 128), BF16),
-            pltpu.VMEM((n, frames // 2, 128), BF16),
-            pltpu.VMEM((total, 128), BF16),
-            pltpu.VMEM((total, 128), F32),
-            pltpu.VMEM((total, 128), F32),
-            pltpu.VMEM((total, 128), F32),
-            pltpu.VMEM((n, frames // 2, 128), BF16),
-            pltpu.VMEM((n, frames // 2, 128), BF16),
-            dma((n,)), dma((n,)), dma((n,)), dma((n,)), dma((n,)), dma((n,)), dma((2,)),
-            dma((Z // 2,)), dma((Z // 2,)), dma((Z // 2,)), dma((Z // 2,)), dma((Z,)), dma((Z,)),
-        ],
-        compiler_params=pltpu.CompilerParams(
-            collective_id=1, has_side_effects=True, vmem_limit_bytes=40 * 2**20
-        ),
-        cost_estimate=pl.CostEstimate(
-            flops=4 * total * total * 16 * 64, bytes_accessed=4 * 2**20, transcendentals=total * total * 16
-        ),
-    )(pk)
+    return jnp.concatenate([kvp, qp], axis=1)
+
+
+def tables(rows, cols):
+    row_start = (lax.axis_index("tm") * lax.axis_size("section") + lax.axis_index("section")) * rows
+    positions = (row_start + jnp.arange(rows, dtype=jnp.int32)).astype(F32)
+    within = jnp.arange(LHD, dtype=jnp.int32)
+    freq = jnp.power(10000.0, -2.0 * (within % (LHD // 2)).astype(F32) / LHD)
+    angle = positions[:, None] * freq[None, :]
+    keys = lax.axis_index("mp") * cols < KVH * LHD
+    sines = jnp.where(within < LHD // 2, -1.0, 1.0) * jnp.sin(angle)
+    return jnp.where(keys, jnp.cos(angle), 1.0), jnp.where(keys, sines, 0.0)
 
 
 def shards(
@@ -313,11 +713,9 @@
     rms_gain,
     kv_weight,
 ):
-    conv2_full, qkv_full, proj_full, kv_full = (
+    conv2_full, qkv_full = (
         lax.all_gather(conv2_weight, "section", axis=1, tiled=True),
         lax.all_gather(qkv_weight, "section", axis=0, tiled=True),
-        lax.all_gather(proj_weight, "section", axis=0, tiled=True),
-        lax.all_gather(kv_weight, "section", axis=0, tiled=True),
     )
     frames_local = mel_frames.shape[0]
     encoded = frames_local // 2
@@ -349,37 +747,23 @@
     projected = jnp.dot(piece, weight_rows, preferred_element_type=jnp.float32).astype(jnp.bfloat16)
     width = qkv_full.shape[2]
     heads = width // HD
-    attended = attention(projected, heads)
-    mixed = lax.psum_scatter(
-        jnp.dot(attended, out_weight, preferred_element_type=jnp.float32).astype(jnp.bfloat16),
-        "mp",
-        scatter_dimension=1,
-        tiled=True,
-    ).astype(jnp.float32)
-    residual = hidden.astype(jnp.float32) + mixed
-    pooled_rows = encoded // 2
-    pooled = jnp.mean(residual.reshape(pooled_rows, 2, channels), axis=1)
-    post = spread_norm(pooled, post_gain).astype(jnp.bfloat16)
-    weight_rows = proj_full
-    embedded = jnp.dot(
-        lax.all_gather(post, "mp", axis=1, tiled=True),
-        weight_rows,
-        preferred_element_type=jnp.float32,
-    ).astype(jnp.bfloat16)
-    widened = embedded.astype(jnp.float32)
-    squares = lax.psum(jnp.sum(widened * widened, axis=-1), "mp")
-    scaled = (widened * lax.rsqrt(squares[:, None] / DL + 1e-06) * rms_gain).astype(jnp.bfloat16)
-    cache = lax.psum_scatter(
-        jnp.dot(scaled, kv_full, preferred_element_type=jnp.float32).astype(jnp.bfloat16),
-        "mp",
-        scatter_dimension=1,
-        tiled=True,
-    ).astype(jnp.float32)
-    row_start = (
-        lax.axis_index("tm") * lax.axis_size("section") + lax.axis_index("section")
-    ) * pooled_rows
-    col_start = lax.axis_index("mp") * cache.shape[1]
-    return rotate_keys(cache, row_start, col_start).astype(jnp.bfloat16)
+    pk = pack(projected, heads)
+    quarter = encoded // 4
+    hq = lax.all_to_all(hidden.reshape(4, quarter, channels), "mp", 0, 0)
+    hq = hq.transpose(1, 0, 2).reshape(quarter, 4 * channels)
+    gains = lax.all_gather(post_gain.reshape(1, channels), "mp", axis=1, tiled=True)
+    cs, sn = tables(encoded // 2, proj_weight.shape[1])
+    return tail(
+        pk,
+        hq,
+        out_weight,
+        proj_weight,
+        kv_weight.reshape(4, kv_weight.shape[0] // 4, kv_weight.shape[1]),
+        gains,
+        rms_gain.reshape(1, -1),
+        cs,
+        sn,
+    )
 
 
 def solution(mesh):

time: 652 us -> 374 us (0.57)
  waiting for transfers between devices: 457 us -> 173 us
  Pallas kernels: 66.1 us -> 109 us
  blocking collectives: 57.1 us -> 29.4 us
  matrix products: 21 us -> 11.7 us
    all_gather x2 -> x0, waiting for transfers between devices: 221 us -> none  [the longest x1 172 us: shards(): lax.all_gather(kv_weight, 'section', axis=0, tiled=True)]
    reduce_scatter x2 -> x0, waiting for transfers between devices: 67.4 us -> none  [the longest x1 37.8 us: shards(): lax.psum_scatter(jnp.dot(scaled, kv_full, preferred_element_type=jnp.floa...]
    pallas_call x1, Pallas kernels: 66.1 us -> 109 us  [tail(): pl.pallas_call(tail_kernel, out_shape=jax.ShapeDtypeStruct((tokens, cols)...]
    psum x1 -> x0, blocking collectives: 14.9 us -> none  [shards(): squares = lax.psum(jnp.sum(widened * widened, axis=-1), 'mp')]
    all_gather x1 -> x0, blocking collectives: 11.2 us -> none  [shards(): lax.all_gather(post, 'mp', axis=1, tiled=True)]
    dot_general x3 -> x0, matrix products: 9.34 us -> none  [the longest x1 5.74 us: shards(): jnp.dot(scaled, kv_full, preferred_element_type=jnp.float32)]
    psum x2 -> x1, blocking collectives: 20.8 us -> 19 us  [spread_norm(): lax.psum((jnp.sum(rows, axis=-1), jnp.sum(rows * rows, axis=-1)), 'mp')]
  transfers between devices with their start and end apart: 10 -> 7, of which waited for: 8 -> 5; matrix products, arithmetic and copies ran while one was open for 4% -> 5% of each run, Pallas kernels for 0% -> 0%
where the time goes in v2:
time: 374 us; the launch traced here: 373 us
  waiting for transfers between devices  173 us (46%)
  Pallas kernels  109 us (29%)
  blocking collectives  29.4 us (8%)
  local copies, waits for them, and re-layouts  19.4 us (5%)
  between operations  14.1 us (4%)
  starting transfers between devices  13.7 us (4%)
  matrix products  11.7 us (3%)
    pallas_call x1, Pallas kernels, tail(): pl.pallas_call(tail_kernel, out_shape=jax.ShapeDtypeStruct((tokens, cols)...  109 us
    all_gather x1, waiting for transfers between devices, shards(): lax.all_gather(conv2_weight, 'section', axis=1, tiled=True)  79.9 us
    all_gather x1, waiting for transfers between devices, shards(): lax.all_gather(qkv_weight, 'section', axis=0, tiled=True)  54.5 us
    all_gather x1, waiting for transfers between devices, shards(): piece = lax.all_gather(extended, 'mp', axis=1, tiled=True)  32.2 us
    psum x1, blocking collectives, spread_norm(): lax.psum((jnp.sum(rows, axis=-1), jnp.sum(rows * rows, axis=-1)), 'mp')  19 us
    all_gather x1, blocking collectives, shards(): piece = lax.all_gather(normed, 'mp', axis=1, tiled=True)  10.4 us
  transfers between devices with their start and end apart: 7, of which 5 were waited for; matrix products, arithmetic and copies ran while one was open for 5% of the time, Pallas kernels for 0%

profile of v2, /device:TPU:1, one launch (start us, length us, event | category | flops | bytes accessed | tf_op | source)
XLA Modules:
  0.0 373.1 jit_solution(4005391642923638397)
XLA Ops:
  6.5 0.7 fusion.46
  7.2 1.3 collective-permute-start.1
  8.5 4.6 %collective-permute-start = (bf16[1,128]{1,0:T(2,128)(2,1)S(1)}, bf16[1,128]{1,0:T(2,128)(2,1)S(1)}, u32[]{:S(2)}, u32[]{:S(2)}) collective-permute-start(bf16[1,128]{1,0:T(2,128)(2,1)S(1)} %get-tuple-element.15), channel_id=1, source_target_pairs={{0,1},{1,2},{2,3},{3,4},{4,5},{5,6},{6,7},{7,8},{8,9},{9,10},{10,1... | collective-permute-start | bytes 776 | tf_op jit(solution)/shard_map/ppermute | solution.py:29
  13.1 1.2 fusion.30
  14.3 1.2 fusion.26
  15.5 2.5 fusion.4
  18.2 4.3 %collective-permute-start.2 = (bf16[1,320]{0,1:T(8,128)(2,1)S(1)}, bf16[1,320]{0,1:T(8,128)(2,1)S(1)}, u32[]{:S(2)}, u32[]{:S(2)}) collective-permute-start(bf16[1,320]{0,1:T(8,128)(2,1)S(1)} %slice.78), channel_id=1, source_target_pairs={{0,1},{1,2},{2,3},{3,4},{4,5},{5,6},{6,7},{7,8},{8,9},{9,10},{10,1... | collective-permute-start | bytes 1928 | tf_op jit(solution)/shard_map/ppermute | solution.py:41
  22.5 1.5 collective-permute-done.2
  24.1 0.9 copy.27
  28.2 1.0 fusion.38
  29.2 32.2 %all-gather.10.cloned.1.call-done = bf16[4,320,513]{1,2,0:T(8,128)(2,1)} async-done(((bf16[1,320,513]{1,2,0:T(8,128)(2,1)}), bf16[4,320,513]{1,2,0:T(8,128)(2,1)}) %all-gather.10.cloned.1.call-update) | async-done | bytes 1313296 | tf_op jit(solution)/shard_map/all_gather | solution.py:734
  61.3 2.0 copy.28
  63.4 2.1 reshape.60
  65.4 1.2 slice.67
  66.6 1.2 slice.69
  67.9 1.5 slice.71
  69.3 54.5 %all-gather.8.cloned.1.call-done = bf16[1280,3,256]{2,0,1:T(8,128)(2,1)} async-done(((bf16[80,3,256]{2,0,1:T(8,128)(2,1)}), bf16[1280,3,256]{2,0,1:T(8,128)(2,1)}) %all-gather.8.cloned.1.call-update) | async-done | bytes 1966096 | tf_op jit(solution)/shard_map/all_gather | solution.py:718
  123.8 4.0 %copy.29 = bf16[1280,3,256]{0,2,1:T(8,128)(2,1)} copy(bf16[1280,3,256]{2,0,1:T(8,128)(2,1)} %all-gather.8.cloned.1.call-done) | data formatting | bytes 3932160 | tf_op jit(solution)/shard_map/all_gather | solution.py:718
  127.8 79.9 %all-gather.6.cloned.1.call-done = bf16[3,1280,320]{2,1,0:T(8,128)(2,1)} async-done(((bf16[3,80,320]{2,1,0:T(8,128)(2,1)}), bf16[3,1280,320]{2,1,0:T(8,128)(2,1)}) %all-gather.6.cloned.1.call-update) | async-done | bytes 2457616 | tf_op jit(solution)/shard_map/all_gather | solution.py:717
  207.7 1.7 fusion.1
  209.4 1.7 convolution_add_fusion.2
  211.2 2.6 convert_reduce_fusion
  213.7 0.8 copy.34
  214.6 19.0 %all-reduce.1 = (f32[256]{0:T(256)S(1)}, f32[256]{0:T(256)S(1)}, f32[1280]{0:T(1024)S(1)}) all-reduce(f32[256]{0:T(256)S(1)} %get-tuple-element.6, f32[256]{0:T(256)S(1)} %get-tuple-element.5, f32[1280]{0:T(1024)S(1)} %dynamic-update-slice), channel_id=1, replica_groups=mesh['tm'=4,'mp'=4,'section'=16] {'mp'}, use_global_device_ids=true, to_apply=%region_3.0 | all-reduce | flops 1792 | bytes 14336 | tf_op jit(solution)/shard_map/psum | solution.py:49
  233.7 10.4 %all_gather.17 = bf16[256,1280]{0,1:T(8,128)(2,1)S(1)} all-gather(bf16[256,320]{0,1:T(8,128)(2,1)S(1)} %fusion.17), channel_id=1, replica_groups=mesh['tm'=4,'mp'=4,'section'=16] {'mp'}, dimensions={1}, use_global_device_ids=true | all-gather | bytes 819200 | tf_op jit(solution)/shard_map/all_gather | solution.py:745
  244.1 0.7 convolution_convert_fusion
  245.6 3.5 all-to-all-start
  249.9 0.8 maximum_maximum_fusion.pk
  250.8 4.0 %all-to-all-done = bf16[4,64,320]{2,1,0:T(8,128)(2,1)S(1)} async-done(((bf16[4,64,320]{2,1,0:T(8,128)(2,1)}), bf16[4,64,320]{2,1,0:T(8,128)(2,1)S(1)}, u32[]{:S(2)}, u32[]{:S(2)}) %all-to-all-start) | async-done | bytes 163872 | tf_op jit(solution)/shard_map/all_to_all | solution.py:752
  254.9 0.8 reshape.51.hq
  255.7 109.1 %shard_map.100 = bf16[128,1024]{1,0:T(8,128)(2,1)} custom-call(bf16[4,384,128]{2,1,0:T(8,128)(2,1)} %maximum_maximum_fusion.pk, bf16[64,1280]{1,0:T(8,128)(2,1)} %reshape.51.hq, bf16[256,1280]{1,0:T(8,128)(2,1)} %ow.1, bf16[80,1024]{1,0:T(8,128)(2,1)} %pw.1, bf16[4,16,4096]{2,1,0:T(8,128)(2,1)} %bitcast.58, f32[1,1280]{1,0:T(1,128)} %reshape.55.pg, ...), custom_call_target="tpu_custom_call" | custom-call | tf_op jit(solution)/shard_map/pallas_call | solution.py:646
  364.9 1.7 copy.41
  (34 shorter events, 4.4 us)
Async XLA Ops:
  6.5 54.8 %all-gather.10.cloned.1.call-start = ((), (), s32[]{:S(2)}) async-start(), calls=%async_computation.3 | async-start | bytes 1996800 | tf_op jit(solution)/shard_map/all_gather | solution.py:734
  7.2 7.1 %collective-permute-start.1 = (bf16[1,128]{1,0:T(2,128)(2,1)S(1)}, bf16[1,128]{1,0:T(2,128)(2,1)S(1)}, u32[]{:S(2)}, u32[]{:S(2)}) collective-permute-start(bf16[1,128]{1,0:T(2,128)(2,1)S(1)} %get-tuple-element.16), channel_id=1, source_target_pairs={{1,0},{2,1},{3,2},{4,3},{5,4},{6,5},{7,6},{8,7},{9,8},{10,9},{11,1... | collective-permute-start | bytes 776 | tf_op jit(solution)/shard_map/ppermute | solution.py:31
  8.5 7.0 %collective-permute-start = (bf16[1,128]{1,0:T(2,128)(2,1)S(1)}, bf16[1,128]{1,0:T(2,128)(2,1)S(1)}, u32[]{:S(2)}, u32[]{:S(2)}) collective-permute-start(bf16[1,128]{1,0:T(2,128)(2,1)S(1)} %get-tuple-element.15), channel_id=1, source_target_pairs={{0,1},{1,2},{2,3},{3,4},{4,5},{5,6},{6,7},{7,8},{8,9},{9,10},{10,1... | collective-permute-start | bytes 776 | tf_op jit(solution)/shard_map/ppermute | solution.py:29
  18.1 8.5 %copy-start.3 = (u32[256]{0:T(256)S(1)}, u32[256]{0:T(256)}, u32[]{:S(2)}) copy-start(u32[256]{0:T(256)} %constant.31) | copy-start | bytes 3076
  18.1 9.8 %copy-start.1 = (f32[320]{0:T(512)S(1)}, f32[320]{0:T(512)}, u32[]{:S(2)}) copy-start(f32[320]{0:T(512)} %param.16) | copy-start | bytes 3844
  18.2 5.7 %collective-permute-start.2 = (bf16[1,320]{0,1:T(8,128)(2,1)S(1)}, bf16[1,320]{0,1:T(8,128)(2,1)S(1)}, u32[]{:S(2)}, u32[]{:S(2)}) collective-permute-start(bf16[1,320]{0,1:T(8,128)(2,1)S(1)} %slice.78), channel_id=1, source_target_pairs={{0,1},{1,2},{2,3},{3,4},{4,5},{5,6},{6,7},{7,8},{8,9},{9,10},{10,1... | collective-permute-start | bytes 1928 | tf_op jit(solution)/shard_map/ppermute | solution.py:41
  25.1 98.7 %all-gather.8.cloned.1.call-start = ((), (), s32[]{:S(2)}) async-start(), calls=%async_computation.2 | async-start | bytes 2088960 | tf_op jit(solution)/shard_map/all_gather | solution.py:718
  25.8 181.9 %all-gather.6.cloned.1.call-start = ((), (), s32[]{:S(2)}) async-start(), calls=%async_computation.1 | async-start | bytes 3133440 | tf_op jit(solution)/shard_map/all_gather | solution.py:717
  211.2 22.4 %copy-start.2 = (f32[320]{0:T(512)S(1)}, f32[320]{0:T(512)}, u32[]{:S(2)}) copy-start(f32[320]{0:T(512)} %param.13) | copy-start | bytes 3844
  211.2 32.9 %copy-start = (bf16[1280,3,256]{0,2,1:T(8,128)(2,1)S(1)}, bf16[1280,3,256]{0,2,1:T(8,128)(2,1)}, u32[]{:S(2)}) copy-start(bf16[1280,3,256]{0,2,1:T(8,128)(2,1)} %copy.29) | copy-start | bytes 5898244
  245.6 9.1 %all-to-all-start = ((bf16[4,64,320]{2,1,0:T(8,128)(2,1)}), bf16[4,64,320]{2,1,0:T(8,128)(2,1)S(1)}, u32[]{:S(2)}, u32[]{:S(2)}) async-start(bf16[4,64,320]{2,1,0:T(8,128)(2,1)} %bitcast.17), calls=%async_computation | async-start | bytes 393216 | tf_op jit(solution)/shard_map/all_to_all | solution.py:752
Sparse Core Ops, SparseCore 0:
  25.2 36.0 all-gather.9
  63.1 60.6 all-gather.7
  125.6 82.0 all-gather.5

commit v3 on v2

--- a/solution.py
+++ b/solution.py
@@ -18,56 +18,6 @@
 BF16 = jnp.bfloat16
 
 
-def extended_2(cells, sides, width):
-    for axis, dim in sides:
-        count = lax.axis_size(axis)
-        ends = count - 1
-        head = lax.slice_in_dim(cells, 0, width, axis=dim)
-        tail = lax.slice_in_dim(cells, cells.shape[dim] - width, cells.shape[dim], axis=dim)
-        cells = jnp.concatenate(
-            [
-                lax.ppermute(tail, axis, [(i, (i + 1) % count) for i in range(ends)]),
-                cells,
-                lax.ppermute(head, axis, [((i + 1) % count, i) for i in range(ends)]),
-            ],
-            axis=dim,
-        )
-    return cells
-
-
-def shifted(value, axis, steps):
-    count = lax.axis_size(axis)
-    initial, last = (max(0, -steps), min(count, count - steps))
-    return lax.ppermute(value, axis, [(source, source + steps) for source in range(initial, last)])
-
-
-def exact_gelu(values):
-    return jax.nn.gelu(values, approximate=False)
-
-
-def spread_norm(rows, gain):
-    sum_rows, sum_squares = lax.psum((jnp.sum(rows, axis=-1), jnp.sum(rows * rows, axis=-1)), "mp")
-    center = sum_rows / D
-    spread = sum_squares / D - center * center
-    return (rows - center[:, None]) * lax.rsqrt(spread[:, None] + 1e-05) * gain
-
-
-def rotate_keys(cache, row_start, col_start):
-    rows_count, cols_count = cache.shape
-    positions = (row_start + jnp.arange(rows_count, dtype=jnp.int32)).astype(jnp.float32)
-    columns = col_start + jnp.arange(cols_count, dtype=jnp.int32)
-    half_size = LHD // 2
-    within = columns % LHD % half_size
-    freq = jnp.power(10000.0, -2.0 * within.astype(jnp.float32) / LHD)
-    angle = positions[:, None] * freq[None, :]
-    grouped = cache.reshape(rows_count, cols_count // LHD, 2, half_size)
-    partner = jnp.stack([-grouped[:, :, 1], grouped[:, :, 0]], axis=2).reshape(
-        rows_count, cols_count
-    )
-    turned = cache * jnp.cos(angle) + partner * jnp.sin(angle)
-    return jnp.where((columns < KVH * LHD)[None, :], turned, cache)
-
-
 def place():
     mp, sec = lax.axis_index("mp"), lax.axis_index("section")
     return lax.axis_index("tm"), mp // 2, mp % 2, sec // 2, sec % 2
@@ -86,6 +36,17 @@
 NEG = -1e30
 TQ = 256
 H0 = 32
+
+
+def line(step, Z, Y):
+    y, x_hi, c, z, x_lo = place()
+    sections = 2 * Z
+    at = lax.rem(y * sections + z * 2 + x_lo + step + Y * sections, Y * sections)
+    return {"tm": at // sections, "mp": x_hi * 2 + c, "section": lax.rem(at, sections)}
+
+
+def gelu(x):
+    return 0.5 * x * (1.0 + lax.erf(x * math.sqrt(0.5)))
 
 
 def greet(Z, Y):
@@ -104,7 +65,8 @@
                 lax.rem(y + dy, Y), lax.rem(x_hi + a, 2), lax.rem(c + b, 2), z, lax.rem(x_lo + d, 2)
             )
             pl.semaphore_signal(barrier, inc=1, device_id=other, device_id_type=MESH)
-    pl.semaphore_wait(barrier, 8 * Y + 1)
+    pl.semaphore_signal(barrier, inc=1, device_id=line(jnp.where(x_lo == 1, 1, -1), Z, Y), device_id_type=MESH)
+    pl.semaphore_wait(barrier, 8 * Y + 2)
 
 
 class Across:
@@ -339,13 +301,14 @@
     return (rows - center) * lax.rsqrt(spread + 1e-05) * gain
 
 
-def tail_kernel(
-    pk, hq, ow, pw, kw, pg, rg, cs, sn, out,
+def layer_kernel(
+    mel, w1, c2, gn, qw, ow, pw, kw, rg, cs, sn, out,
+    hprev, hnext, w1f, gf, c2f, qwf, xe, even, odd, hbox, nbuf, pk,
     kv, qbox, qs, m, l, acc, obuf, abox, att, res, owf, pwf, kwf, pbox, sbox, keep, tsend, trecv, csend, crecv,
     kv_s, kv_r, q_s, q_r, loc, up_s, up_r, dn_s, dn_r, co_s, co_r, a_s, a_r,
     ow_s, ow_r, pb_s, pb_r, sb_s, sb_r, t_s, t_r, c_s, c_r,
-    p0, p1, p2, p3, p4, p5, p6, p7, p8, p9,
-    k0, k1, k2, k3, k4, k5, k6, k7, k8, k9, k10, k11, k12, k13,
+    h_s, h_r, w1_s, w1_r, g_s, g_r, hb_s, hb_r,
+    *rings,
 ):
     y, x_hi, c, z, x_lo = place()
     Z = kv.shape[0]
@@ -357,11 +320,111 @@
     far_dev = device(y, 1 - x_hi, c, z, x_lo)
     peers = [device(i, x_hi, x_lo, z, c) for i in range(n)]
     mirror = c == x_lo
+
+    outw = Across(ow, owf, ow_s, ow_r)
+    proj = Sections(pw, pwf, *rings[0:10], loc.at[3], H0)
+    conv = Sections(c2, c2f, *rings[10:20], loc.at[6], 96)
+    qkv = Sections(qw, qwf, *rings[20:30], loc.at[7], H0)
+    kvw = Quarters(kw, kwf, *rings[30:44], loc.at[4])
+    first_w = Across(w1, w1f, w1_s, w1_r)
+    gains = Across(gn, gf, g_s, g_r)
+    own_w1 = pltpu.make_async_copy(w1, w1f.at[me], loc.at[8])
+    own_g = pltpu.make_async_copy(gn, gf.at[me], loc.at[9])
+    own_w1.start()
+    own_g.start()
+    count = mel.shape[0]
     greet(Z, n)
 
-    outw = Across(ow, owf, ow_s, ow_r)
-    proj = Sections(pw, pwf, p0, p1, p2, p3, p4, p5, p6, p7, p8, p9, loc.at[3], H0)
-    kvw = Quarters(kw, kwf, k0, k1, k2, k3, k4, k5, k6, k7, k8, k9, k10, k11, k12, k13, loc.at[4])
+    tail16, head16 = pl.ds(count - 16, 16), pl.ds(0, 16)
+    edge_next = remote(mel.at[tail16], hprev, h_s.at[0], h_r.at[0], line(1, Z, n))
+    edge_prev = remote(mel.at[head16], hnext, h_s.at[1], h_r.at[1], line(-1, Z, n))
+    first_w.start()
+    edge_next.start()
+    edge_prev.start()
+    conv.start()
+    gains.start()
+    conv.start_other()
+    first_w.relay()
+    gains.relay()
+    edge_next.wait_recv()
+    edge_prev.wait_recv()
+    block_at = y * 2 * Z + z * 2 + x_lo
+    begins = jnp.where(block_at == 0, 0.0, 1.0)
+    ends = jnp.where(block_at == 2 * Z * n - 1, 0.0, 1.0)
+    xe[0:16, :] = hprev[...].astype(F32) * begins
+    xe[16 : 16 + count, :] = mel[...].astype(F32)
+    xe[16 + count :, :] = hnext[...].astype(F32) * ends
+    left = jnp.concatenate(
+        [xe[15 : 15 + count, 128:256], xe[16 : 16 + count, :]], axis=1
+    ).astype(BF16)
+    right = jnp.concatenate([xe[0 : 16 + count, :], xe[1 : 17 + count, 0:128]], axis=1).astype(BF16)
+    inside = jnp.where(
+        lax.broadcasted_iota(jnp.int32, (16 + count, 1), 0) >= 16, jnp.ones((16 + count, 1), F32), begins
+    )
+    own_w1.wait()
+    first_w.finish()
+    for part in range(4):
+        even[part] = gelu(jnp.dot(left, w1f[part], preferred_element_type=F32)).astype(BF16)
+        odd[part] = gelu(jnp.dot(right, w1f[part], preferred_element_type=F32)) * inside
+        if part == 1:
+            conv.step(1)
+    conv.step(2)
+    qkv.start()
+    conv.step(3)
+    qkv.start_other()
+    conv.step(Z // 2)
+    kvw.start()
+    own_w = pltpu.make_async_copy(ow, owf.at[me], loc.at[5])
+    own_w.start()
+    conv.finish()
+
+    rows2 = c2.shape[0] // 3
+    wide = w1.shape[1]
+    second = jnp.zeros((count, wide), F32)
+    for part in range(4):
+        taps = (
+            odd[part, 15 : 15 + count, :].astype(BF16),
+            even[part],
+            odd[part, 16 : 16 + count, :].astype(BF16),
+        )
+        for tap in range(3):
+            w = c2f[2 * part : 2 * part + 2, :, tap * rows2 : (tap + 1) * rows2, :].reshape(4 * rows2, wide)
+            second = second + jnp.dot(taps[tap], w, preferred_element_type=F32)
+    hbox[me] = gelu(second).astype(BF16)
+    share_h = Across(hbox.at[me], hbox, hb_s, hb_r)
+    share_h.start()
+    qkv.step(1)
+    share_h.relay()
+    qkv.step(2)
+    own_g.wait()
+    gains.finish()
+    share_h.finish()
+    parts = [hbox[k].astype(F32) for k in range(4)]
+    center = sum(jnp.sum(p, axis=1, keepdims=True) for p in parts) / D
+    parts = [p - center for p in parts]
+    inv = lax.rsqrt(sum(jnp.sum(p * p, axis=1, keepdims=True) for p in parts) / D + 1e-05)
+    for k in range(4):
+        nbuf[k] = (parts[k] * inv * gf[k, 0:1, :]).astype(BF16)
+    qkv.step(3)
+    kvw.begin()
+    qkv.step(Z // 2)
+    qkv.finish()
+    projected = jnp.zeros((count, qw.shape[1]), F32)
+    for k in range(4):
+        projected = projected + jnp.dot(
+            nbuf[k], qwf[2 * k : 2 * k + 2].reshape(4 * qw.shape[0], qw.shape[1]), preferred_element_type=F32
+        )
+    split = count // 2
+    lower = lax.broadcasted_iota(jnp.int32, (split, 128), 1) < HD
+    for i in range(n):
+        pk[i, 0:count, :] = projected[:, i * 128 : (i + 1) * 128].astype(BF16)
+        at = n * 128 + (i // 2) * 128
+        a, b = projected[0:split, at : at + 128], projected[split:, at : at + 128]
+        if i % 2 == 0:
+            mixed_q = jnp.where(lower, a, pltpu.roll(b, HD, 1))
+        else:
+            mixed_q = jnp.where(lower, pltpu.roll(a, HD, 1), b)
+        pk[i, count:, :] = mixed_q.astype(BF16)
 
     half = kv.shape[2] // n
     for i in range(n):
@@ -377,10 +440,6 @@
         def _():
             pltpu.make_async_copy(pk.at[i, 0:half], kv.at[z, c, rows], loc.at[0]).start()
             pltpu.make_async_copy(pk.at[i, half:], qbox.at[y], loc.at[1]).start()
-
-    kvw.start()
-    own_w = pltpu.make_async_copy(ow, owf.at[me], loc.at[5])
-    own_w.start()
 
     m[...] = jnp.full(m.shape, NEG, F32)
     l[...] = jnp.zeros(l.shape, F32)
@@ -454,7 +513,6 @@
 
         lax.fori_loop(0, total // TQ, tile, 0)
 
-    kvw.begin()
     process(z, c)
     taken(0, z).wait_recv()
     process(z, 1 - c)
@@ -561,14 +619,17 @@
     )
     tokens = quarter // 2
     pieces = []
-    for k in range(hq.shape[1] // 128):
+    mine = pl.ds(pl.multiple_of(me * quarter, quarter), quarter)
+    own_rows = jnp.concatenate([hbox[k, mine, :].astype(F32) for k in range(4)], axis=1)
+    gain = jnp.concatenate([gf[k, 1:2, :] for k in range(4)], axis=1)
+    for k in range(D // 128):
         at = slice(k * 128, (k + 1) * 128)
-        res[k] = hq[:, at].astype(F32) + mixed[:, at]
+        res[k] = own_rows[:, at] + mixed[:, at]
         pieces.append(
             (res.at[k][pl.ds(0, tokens, stride=2), :] + res.at[k][pl.ds(1, tokens, stride=2), :]) * 0.5
         )
     pooled = jnp.concatenate(pieces, axis=1)
-    pbox[me] = normal(pooled, pg[0:1, :]).astype(BF16)
+    pbox[me] = normal(pooled, gain).astype(BF16)
     gather = Across(pbox.at[me], pbox, pb_s, pb_r)
     gather.start()
     gather.relay()
@@ -619,6 +680,8 @@
         value = (keep[:, at] + crecv[:, at].astype(F32)) * scale
         out[:, at] = (value * cs[...] + pltpu.roll(value, HD, 1) * sn[...]).astype(BF16)
 
+    edge_next.wait_send()
+    edge_prev.wait_send()
     swap(0).wait_send()
     swap(1).wait_send()
     over.wait_send()
@@ -631,24 +694,38 @@
                 give(j, q, head, head).wait_send()
 
 
-def tail(pk, hq, ow, pw, kw, pg, rg, cs, sn):
-    n = pk.shape[0]
-    frames = pk.shape[1] * 2 // 3
+def layer(mel, w1, c2, gn, qw, ow, pw, kw, rg, cs, sn):
+    frames = mel.shape[0]
+    n = lax.axis_size("tm")
     Z = lax.axis_size("section") // 2
     total = frames * n
     tokens = frames // 2
     quarter = frames // 4
     cols = pw.shape[1]
+    wide = w1.shape[1]
     sem = pltpu.SemaphoreType.DMA
     vm = pl.BlockSpec(memory_space=pltpu.VMEM)
     V = pltpu.VMEM
     half = Z // 2
+    ring = [sem((half,))] * 8 + [sem((Z,))] * 2
     return pl.pallas_call(
-        tail_kernel,
+        layer_kernel,
         out_shape=jax.ShapeDtypeStruct((tokens, cols), BF16),
-        in_specs=[vm] * 9,
+        in_specs=[vm] * 11,
         out_specs=vm,
         scratch_shapes=[
+            V((16, mel.shape[1]), BF16),
+            V((16, mel.shape[1]), BF16),
+            V((4,) + w1.shape, BF16),
+            V((4,) + gn.shape, F32),
+            V((Z, 2) + c2.shape, BF16),
+            V((Z, 2) + qw.shape, BF16),
+            V((frames + 32, mel.shape[1]), F32),
+            V((4, frames, wide), BF16),
+            V((4, frames + 16, wide), F32),
+            V((4, frames, wide), BF16),
+            V((4, frames, wide), BF16),
+            V((n, frames + tokens, 128), BF16),
             V((Z, 2, total, 128), BF16),
             V((n, tokens, 128), BF16),
             V((total, 128), BF16),
@@ -669,25 +746,17 @@
             V((2, tokens, cols), BF16),
             V((tokens, cols), BF16),
             V((tokens, cols), BF16),
-            sem((n,)), sem((n,)), sem((n,)), sem((n,)), sem((6,)),
+            sem((n,)), sem((n,)), sem((n,)), sem((n,)), sem((10,)),
             sem((half,)), sem((half,)), sem((half,)), sem((half,)), sem((Z,)), sem((Z,)), sem((16,)), sem((16,)),
             sem((3,)), sem((3,)), sem((3,)), sem((3,)), sem((3,)), sem((3,)), sem((2,)), sem((2,)), sem((1,)), sem((1,)),
+            sem((2,)), sem((2,)), sem((3,)), sem((3,)), sem((3,)), sem((3,)), sem((3,)), sem((3,)),
         ]
-        + [sem((half,))] * 8 + [sem((Z,))] * 2
+        + ring * 3
         + [sem((half,))] * 4 + [sem((1,))] * 2 + [sem((Z,))] * 8,
         compiler_params=pltpu.CompilerParams(
-            collective_id=1, has_side_effects=True, vmem_limit_bytes=56 * 2**20
+            collective_id=1, has_side_effects=True, vmem_limit_bytes=60 * 2**20
         ),
-    )(pk, hq, ow, pw, kw, pg, rg, cs, sn)
-
-
-def pack(projected, heads):
-    frames = projected.shape[0]
-    split = projected.reshape(frames, 3, heads, HD)
-    kvp = jnp.concatenate([split[:, 1], split[:, 2]], axis=-1).transpose(1, 0, 2)
-    q = split[:, 0].transpose(1, 0, 2)
-    qp = jnp.concatenate([q[:, : frames // 2], q[:, frames // 2 :]], axis=-1)
-    return jnp.concatenate([kvp, qp], axis=1)
+    )(mel, w1, c2, gn, qw, ow, pw, kw, rg, cs, sn)
 
 
 def tables(rows, cols):
@@ -713,53 +782,24 @@
     rms_gain,
     kv_weight,
 ):
-    conv2_full, qkv_full = (
-        lax.all_gather(conv2_weight, "section", axis=1, tiled=True),
-        lax.all_gather(qkv_weight, "section", axis=0, tiled=True),
-    )
-    frames_local = mel_frames.shape[0]
-    encoded = frames_local // 2
-    channels = conv1_weight.shape[2]
-    padded = extended_2(mel_frames, ((("tm", "section"), 0),), 1)
-    first_sum = jnp.dot(padded[0:frames_local], conv1_weight[0], preferred_element_type=jnp.float32)
-    first_sum = first_sum + jnp.dot(
-        padded[1 : frames_local + 1], conv1_weight[1], preferred_element_type=jnp.float32
-    )
-    first_sum = first_sum + jnp.dot(
-        padded[2 : frames_local + 2], conv1_weight[2], preferred_element_type=jnp.float32
-    )
-    first = exact_gelu(first_sum).astype(jnp.bfloat16)
-    before = shifted(first[frames_local - 1 :], ("tm", "section"), 1)
-    extended = jnp.concatenate([before, first], axis=0)
-    piece = lax.all_gather(extended, "mp", axis=1, tiled=True)
-    state = jnp.dot(piece[0:frames_local:2], conv2_full[0], preferred_element_type=jnp.float32)
-    state = state + jnp.dot(
-        piece[1 : frames_local + 1 : 2], conv2_full[1], preferred_element_type=jnp.float32
-    )
-    second = state + jnp.dot(
-        piece[2 : frames_local + 2 : 2], conv2_full[2], preferred_element_type=jnp.float32
-    )
-    hidden = exact_gelu(second).astype(jnp.bfloat16)
-    normed = spread_norm(hidden.astype(jnp.float32), attn_gain).astype(jnp.bfloat16)
-    qkv_cols = qkv_full.shape[1] * qkv_full.shape[2]
-    piece = lax.all_gather(normed, "mp", axis=1, tiled=True)
-    weight_rows = qkv_full.reshape(piece.shape[1], qkv_cols)
-    projected = jnp.dot(piece, weight_rows, preferred_element_type=jnp.float32).astype(jnp.bfloat16)
-    width = qkv_full.shape[2]
+    frames = mel_frames.shape[0] // 2
+    bins, wide = conv1_weight.shape[1:]
+    rows, _, width = qkv_weight.shape
     heads = width // HD
-    pk = pack(projected, heads)
-    quarter = encoded // 4
-    hq = lax.all_to_all(hidden.reshape(4, quarter, channels), "mp", 0, 0)
-    hq = hq.transpose(1, 0, 2).reshape(quarter, 4 * channels)
-    gains = lax.all_gather(post_gain.reshape(1, channels), "mp", axis=1, tiled=True)
-    cs, sn = tables(encoded // 2, proj_weight.shape[1])
-    return tail(
-        pk,
-        hq,
+    split = qkv_weight.reshape(rows, 3, heads, HD)
+    pairs = jnp.stack([split[:, 1], split[:, 2]], axis=2).reshape(rows, 2 * width)
+    weight = jnp.concatenate([pairs, qkv_weight[:, 0]], axis=1)
+    gains = jnp.pad(jnp.stack([attn_gain, post_gain]), ((0, 6), (0, 0)))
+    cs, sn = tables(frames // 2, proj_weight.shape[1])
+    return layer(
+        mel_frames.reshape(frames, 2 * bins),
+        conv1_weight.reshape(3 * bins, wide),
+        conv2_weight.reshape(-1, wide),
+        gains,
+        weight,
         out_weight,
         proj_weight,
         kv_weight.reshape(4, kv_weight.shape[0] // 4, kv_weight.shape[1]),
-        gains,
         rms_gain.reshape(1, -1),
         cs,
         sn,

time: 374 us -> 187 us (0.50)
  waiting for transfers between devices: 173 us -> 0 us
  Pallas kernels: 109 us -> 179 us
  blocking collectives: 29.4 us -> 0 us
  local copies, waits for them, and re-layouts: 19.4 us -> 5.37 us
  between operations: 14.1 us -> 0.08 us
  starting transfers between devices: 13.7 us -> 0 us
  matrix products: 11.7 us -> 0 us
    all_gather x3 -> x0, waiting for transfers between devices: 167 us -> none  [the longest x1 79.9 us: shards(): lax.all_gather(conv2_weight, 'section', axis=1, tiled=True)]
    pallas_call x1, Pallas kernels: 109 us -> 179 us  [layer(): pl.pallas_call(layer_kernel, out_shape=jax.ShapeDtypeStruct((tokens, cols...]
    psum x1 -> x0, blocking collectives: 19 us -> none  [spread_norm(): lax.psum((jnp.sum(rows, axis=-1), jnp.sum(rows * rows, axis=-1)), 'mp')]
    dot_general x7 -> x0, matrix products: 11.7 us -> none  [the longest x1 2.56 us: shards(): jnp.dot(piece[2:frames_local + 2:2], conv2_full[2], preferred_element_typ...]
    all_gather x1 -> x0, blocking collectives: 10.4 us -> none  [shards(): piece = lax.all_gather(normed, 'mp', axis=1, tiled=True)]
    ppermute x3 -> x0, starting transfers between devices: 10.1 us -> none  [the longest x1 4.56 us: extended_2(): lax.ppermute(tail, axis, [(i, (i + 1) % count) for i in range(ends)])]
    all_gather x3 -> x0, local copies, waits for them, and re-layouts: 6.61 us -> none  [the longest x1 3.99 us: shards(): lax.all_gather(qkv_weight, 'section', axis=0, tiled=True)]
    slice x7 -> x0, local copies, waits for them, and re-layouts: 4.73 us -> none  [the longest x1 1.47 us: shards(): piece[2:frames_local + 2:2]]
  transfers between devices with their start and end apart: 7 -> 0, of which waited for: 5 -> 0; matrix products, arithmetic and copies ran while one was open for 5% -> 0% of each run, Pallas kernels for 0% -> 0%
where the time goes in v3:
time: 187 us
  Pallas kernels  179 us (96%)
  local copies, waits for them, and re-layouts  5.37 us (3%)
  other arithmetic  2.27 us (1%)
    pallas_call x1, Pallas kernels, layer(): pl.pallas_call(layer_kernel, out_shape=jax.ShapeDtypeStruct((tokens, cols...  179 us
    unnamed x13, local copies, waits for them, and re-layouts  3.76 us

profile of v3, /device:TPU:1, one launch (start us, length us, event | category | flops | bytes accessed | tf_op | source)
XLA Modules:
  0.0 186.7 jit_solution(2533130178240120753)
XLA Ops:
  0.0 0.0 copy-start.3
  0.0 0.0 copy-start.4
  0.0 0.0 copy-start.2
  0.0 0.6 copy-done.3
  0.7 0.0 copy-done.4
  0.7 0.6 select_maximum_fusion.gn
  1.3 0.8 slice_bitcast_fusion.2
  2.1 1.0 fusion.2
  3.1 0.0 copy-done.2
  3.1 0.0 copy-start.1
  3.1 0.7 reshape.43.mel
  3.8 0.2 copy-done.1
  4.0 0.2 copy.14
  4.2 0.0 copy-start
  4.2 0.1 copy.17
  4.3 0.7 pad_maximum_fusion.1.qw
  5.0 0.2 copy-done
  5.2 0.9 copy.13
  6.0 179.0 %shard_map.100 = bf16[128,1024]{1,0:T(8,128)(2,1)} custom-call(bf16[256,256]{1,0:T(8,128)(2,1)} %reshape.43.mel, bf16[384,320]{1,0:T(8,128)(2,1)} %bitcast.14, bf16[240,320]{1,0:T(8,128)(2,1)} %bitcast.18, f32[8,320]{1,0:T(8,128)} %select_maximum_fusion.gn, bf16[80,768]{1,0:T(8,128)(2,1)} %pad_maximum_fusion.1.qw, bf16[256,1280]{1,0:T(8,128)(2,1)} %ow.1, ...), custom_call_target="tpu_custom_call" | custom-call | tf_op jit(solution)/shard_map/pallas_call | solution.py:711
  185.0 1.7 copy.19
  (7 shorter events, 0.1 us)
Async XLA Ops:
  0.0 0.7 copy-start.3
  0.0 0.7 copy-start.4
  0.0 3.1 %copy-start.2 = (bf16[512,128]{1,0:T(8,128)(2,1)S(1)}, bf16[512,128]{1,0:T(8,128)(2,1)}, u32[]{:S(2)}) copy-start(bf16[512,128]{1,0:T(8,128)(2,1)} %param.10) | copy-start | bytes 393220
  3.1 0.9 copy-start.1
  4.2 0.9 copy-start

commit v4 on v3

--- a/solution.py
+++ b/solution.py
@@ -34,8 +34,8 @@
 
 
 NEG = -1e30
-TQ = 256
-H0 = 32
+BY_Y = 128
+ROWS_Y = 64
 
 
 def line(step, Z, Y):
@@ -70,14 +70,14 @@
 
 
 class Across:
-    def __init__(self, src, buf, send, recv):
+    def __init__(self, src, buf, send, recv, near=False):
         y, x_hi, c, z, x_lo = place()
         self.buf, self.send, self.recv, self.src = buf, send, recv, src
         self.me, self.twin, self.far, self.both = (
             x_hi * 2 + c, x_hi * 2 + 1 - c, (1 - x_hi) * 2 + c, (1 - x_hi) * 2 + 1 - c
         )
         self.to_twin = device(y, x_hi, 1 - c, z, x_lo)
-        self.to_far = device(y, 1 - x_hi, c, z, x_lo)
+        self.to_far = device(y, 1 - x_hi, c, z, 1 - x_lo if near else x_lo)
 
     def copy(self, k, src, slot, target):
         return remote(src, self.buf.at[slot], self.send.at[k], self.recv.at[k], target)
@@ -197,19 +197,25 @@
 
 
 class Quarters:
-    def __init__(self, src, buf, us, ur, ds, dr, xs, xr, yus, yur, yds, ydr, rus, rur, rds, rdr, loc):
+    def __init__(self, src, buf, us, ur, ds, dr, xs, xr, yus, yur, yds, ydr, rus, rur, rds, rdr, loc, other=None, Y=4):
         y, x_hi, c, z, x_lo = place()
-        self.Z, self.Y = buf.shape[0], buf.shape[2]
-        self.src, self.buf, self.z, self.x, self.y = src, buf, z, x_lo, y
+        self.Z, self.Y = buf.shape[0], Y
+        self.rows = buf.shape[2] // Y
+        self.other = src if other is None else other
+        self.src, self.buf, self.z, self.x, self.y = src, buf, z, x_lo, y if Y > 1 else 0
         self.s = (us, ur, ds, dr, xs, xr, yus, yur, yds, ydr, rus, rur, rds, rdr)
         self.loc = loc
         self.up = device(y, x_hi, c, lax.rem(z + 1, self.Z), x_lo)
         self.down = device(y, x_hi, c, lax.rem(z + self.Z - 1, self.Z), x_lo)
         self.side = device(y, x_hi, c, z, 1 - x_lo)
-        self.yn, self.yp = lax.rem(y + 1, self.Y), lax.rem(y + self.Y - 1, self.Y)
-        self.yf = lax.rem(y + 2, self.Y)
+        self.yn, self.yp, self.yf = lax.rem(y + 1, 4), lax.rem(y + 3, 4), lax.rem(y + 2, 4)
         self.next = device(self.yn, x_hi, c, z, x_lo)
         self.prev = device(self.yp, x_hi, c, z, x_lo)
+
+    def part(self, q):
+        if self.Y == 1:
+            return pl.ds(0, self.rows)
+        return pl.ds(pl.multiple_of(q * self.rows, self.rows), self.rows)
 
     def zs(self, k):
         if k % 2:
@@ -218,14 +224,15 @@
 
     def ring(self, kind, t, zz):
         us, ur, ds, dr = self.s[:4]
-        ref = self.buf.at[zz, :, self.y]
+        ref = self.buf.at[zz, :, self.part(self.y)]
         if kind == "u":
             return remote(ref, ref, us.at[t], ur.at[t], self.up)
         return remote(ref, ref, ds.at[t], dr.at[t], self.down)
 
     def cross(self, x):
         xs, xr = self.s[4:6]
-        return remote(self.src.at[self.y], self.buf.at[self.z, x, self.y], xs.at[0], xr.at[0], self.side)
+        at = self.part(self.y)
+        return remote(self.other.at[at], self.buf.at[self.z, x, at], xs.at[0], xr.at[0], self.side)
 
     def local(self):
         return pltpu.make_async_copy(self.src, self.buf.at[self.z, self.x], self.loc)
@@ -233,9 +240,9 @@
     def spread(self, kind, k, quarter):
         yus, yur, yds, ydr = self.s[6:10]
         if k == 0:
-            ref = self.buf.at[self.z, 1 - self.x, quarter]
+            ref = self.buf.at[self.z, 1 - self.x, self.part(quarter)]
         else:
-            ref = self.buf.at[self.zs(k), :, quarter]
+            ref = self.buf.at[self.zs(k), :, self.part(quarter)]
         if kind == "n":
             return remote(ref, ref, yus.at[k], yur.at[k], self.next)
         return remote(ref, ref, yds.at[k], ydr.at[k], self.prev)
@@ -243,9 +250,9 @@
     def relay(self, kind, k, quarter):
         rus, rur, rds, rdr = self.s[10:14]
         if kind == "n":
-            ref = self.buf.at[self.zs(k), (1 - self.x) if k == 0 else 0, quarter]
+            ref = self.buf.at[self.zs(k), (1 - self.x) if k == 0 else 0, self.part(quarter)]
             return remote(ref, ref, rus.at[k], rur.at[k], self.next)
-        ref = self.buf.at[self.zs(k), 1, quarter]
+        ref = self.buf.at[self.zs(k), 1, self.part(quarter)]
         return remote(ref, ref, rds.at[k], rdr.at[k], self.prev)
 
     def start(self):
@@ -255,19 +262,27 @@
     def begin(self):
         self.local().wait()
         self.cross(1 - self.x).wait_recv()
-        self.spread("n", 0, self.y).start()
-        self.spread("p", 0, self.y).start()
         self.ring("u", 0, self.z).start()
         self.ring("d", 0, self.z).start()
+        if self.Y > 1:
+            self.spread("n", 0, self.y).start()
+            self.spread("p", 0, self.y).start()
+
+    def fetch(self, k):
+        self.ring("u" if k % 2 else "d", (k + 1) // 2 - 1, self.zs(k)).wait_recv()
+        if self.Y > 1:
+            self.spread("n", k, self.y).start()
+            self.spread("p", k, self.y).start()
+
+    def onward(self, k):
+        far, t = self.Z // 2, (k + 1) // 2
+        kind = "u" if k % 2 else "d"
+        if t < (far if kind == "u" else far - 1):
+            self.ring(kind, t, self.zs(k)).start()
 
     def arrive(self, k):
-        far, t, zz = self.Z // 2, (k + 1) // 2, self.zs(k)
-        kind = "u" if k % 2 else "d"
-        self.ring(kind, t - 1, zz).wait_recv()
-        if t < (far if kind == "u" else far - 1):
-            self.ring(kind, t, zz).start()
-        self.spread("n", k, self.y).start()
-        self.spread("p", k, self.y).start()
+        self.fetch(k)
+        self.onward(k)
 
     def pass_on(self, k):
         self.spread("n", k, self.yp).wait_recv()
@@ -278,7 +293,8 @@
 
     def finish(self):
         far = self.Z // 2
-        for k in range(2 * far):
+        turns = range(2 * far if self.Y > 1 else 0)
+        for k in turns:
             self.relay("n", k, self.yf).wait_recv()
             if k:
                 self.relay("p", k, self.yf).wait_recv()
@@ -287,7 +303,7 @@
             self.ring("u", t, self.z).wait_send()
         for t in range(far - 1):
             self.ring("d", t, self.z).wait_send()
-        for k in range(2 * far):
+        for k in turns:
             self.spread("n", k, self.y).wait_send()
             self.spread("p", k, self.y).wait_send()
             self.relay("n", k, self.y).wait_send()
@@ -303,10 +319,10 @@
 
 def layer_kernel(
     mel, w1, c2, gn, qw, ow, pw, kw, rg, cs, sn, out,
-    hprev, hnext, w1f, gf, c2f, qwf, xe, even, odd, hbox, nbuf, pk,
-    kv, qbox, qs, m, l, acc, obuf, abox, att, res, owf, pwf, kwf, pbox, sbox, keep, tsend, trecv, csend, crecv,
+    hprev, hnext, w1f, gf, c2f, c2y, qwy, qwz, kwa, xe, even, odd, hbox, nbuf, pk,
+    kv, qbox, qs, m, l, acc, obuf, abox, att, res, owf, pwy, pwz, kwf, pbox, sbox, ebox, keep, tsend, trecv, csend, crecv, psend, precv,
     kv_s, kv_r, q_s, q_r, loc, up_s, up_r, dn_s, dn_r, co_s, co_r, a_s, a_r,
-    ow_s, ow_r, pb_s, pb_r, sb_s, sb_r, t_s, t_r, c_s, c_r,
+    ow_s, ow_r, pb_s, pb_r, sb_s, sb_r, t_s, t_r, c_s, c_r, e_s, e_r,
     h_s, h_r, w1_s, w1_r, g_s, g_r, hb_s, hb_r,
     *rings,
 ):
@@ -321,31 +337,59 @@
     peers = [device(i, x_hi, x_lo, z, c) for i in range(n)]
     mirror = c == x_lo
 
-    outw = Across(ow, owf, ow_s, ow_r)
-    proj = Sections(pw, pwf, *rings[0:10], loc.at[3], H0)
-    conv = Sections(c2, c2f, *rings[10:20], loc.at[6], 96)
-    qkv = Sections(qw, qwf, *rings[20:30], loc.at[7], H0)
-    kvw = Quarters(kw, kwf, *rings[30:44], loc.at[4])
-    first_w = Across(w1, w1f, w1_s, w1_r)
-    gains = Across(gn, gf, g_s, g_r)
+    outw = Across(ow, owf, ow_s, ow_r, True)
+    quarters, pairs = rings[10:66], rings[66:78]
+    none = (None,) * 8
+    proj_y = Quarters(pw.at[pl.ds(0, ROWS_Y)], pwy, *quarters[0:14], loc.at[3])
+    proj_z = Quarters(pw.at[pl.ds(ROWS_Y, pw.shape[0] - ROWS_Y)], pwz, *pairs[0:6], *none, loc.at[10], Y=1)
+    qkv_y = Quarters(qw.at[pl.ds(0, ROWS_Y)], qwy, *quarters[14:28], loc.at[7])
+    qkv_z = Quarters(qw.at[pl.ds(ROWS_Y, qw.shape[0] - ROWS_Y)], qwz, *pairs[6:12], *none, loc.at[11], Y=1)
+    conv = Sections(c2.at[pl.ds(BY_Y, c2.shape[0] - BY_Y)], c2f, *rings[0:10], loc.at[6], 48)
+    conv_y = Quarters(c2.at[pl.ds(0, BY_Y)], c2y, *quarters[28:42], loc.at[2])
+    kvw = Quarters(kwa.at[x_lo], kwf, *quarters[42:56], loc.at[4], kwa.at[1 - x_lo])
+    first_w = Across(w1, w1f, w1_s, w1_r, True)
+    gains = Across(gn, gf, g_s, g_r, True)
     own_w1 = pltpu.make_async_copy(w1, w1f.at[me], loc.at[8])
     own_g = pltpu.make_async_copy(gn, gf.at[me], loc.at[9])
     own_w1.start()
     own_g.start()
+    wide_c = kw.shape[1] // 8
+    arrange = [
+        pltpu.make_async_copy(
+            kw.at[:, pl.ds((2 * k + h) * wide_c, wide_c)], kwa.at[h, :, pl.ds(k * wide_c, wide_c)], loc.at[12 + 4 * h + k]
+        )
+        for h in range(2)
+        for k in range(4)
+    ]
+    for copy in arrange:
+        copy.start()
     count = mel.shape[0]
     greet(Z, n)
 
     tail16, head16 = pl.ds(count - 16, 16), pl.ds(0, 16)
     edge_next = remote(mel.at[tail16], hprev, h_s.at[0], h_r.at[0], line(1, Z, n))
     edge_prev = remote(mel.at[head16], hnext, h_s.at[1], h_r.at[1], line(-1, Z, n))
+    conv_y.start()
+    conv.start()
     first_w.start()
     edge_next.start()
     edge_prev.start()
-    conv.start()
     gains.start()
+    qkv_y.start()
+    qkv_z.start()
+    conv_y.begin()
     conv.start_other()
+    qkv_y.begin()
+    qkv_z.begin()
     first_w.relay()
     gains.relay()
+    for copy in arrange:
+        copy.wait()
+    kvw.start()
+    proj_y.start()
+    proj_z.start()
+    own_w = pltpu.make_async_copy(ow, owf.at[me], loc.at[5])
+    own_w.start()
     edge_next.wait_recv()
     edge_prev.wait_recv()
     block_at = y * 2 * Z + z * 2 + x_lo
@@ -366,17 +410,47 @@
     for part in range(4):
         even[part] = gelu(jnp.dot(left, w1f[part], preferred_element_type=F32)).astype(BF16)
         odd[part] = gelu(jnp.dot(right, w1f[part], preferred_element_type=F32)) * inside
-        if part == 1:
+        if part == 0:
+            conv_y.arrive(1)
+            conv_y.arrive(2)
             conv.step(1)
-    conv.step(2)
-    qkv.start()
+            for k in (1, 2):
+                qkv_y.arrive(k)
+                qkv_z.arrive(k)
+            conv_y.pass_on(0)
+            qkv_y.pass_on(0)
+        if part == 2:
+            conv_y.arrive(3)
+            conv_y.arrive(4)
+            conv.step(2)
+            for k in (3, 4):
+                qkv_y.arrive(k)
+                qkv_z.arrive(k)
+            conv_y.pass_on(1)
+            conv_y.pass_on(2)
+    conv_y.arrive(5)
+    conv_y.arrive(6)
     conv.step(3)
-    qkv.start_other()
+    for k in (5, 6):
+        qkv_y.arrive(k)
+        qkv_z.arrive(k)
+    conv_y.pass_on(3)
+    conv_y.pass_on(4)
+    qkv_y.pass_on(1)
+    qkv_y.pass_on(2)
+    kvw.begin()
+    conv_y.arrive(7)
     conv.step(Z // 2)
-    kvw.start()
-    own_w = pltpu.make_async_copy(ow, owf.at[me], loc.at[5])
-    own_w.start()
+    qkv_y.arrive(7)
+    qkv_z.arrive(7)
+    for k in (5, 6, 7):
+        conv_y.pass_on(k)
+    qkv_y.pass_on(3)
+    qkv_y.pass_on(4)
+    proj_y.begin()
+    proj_z.begin()
     conv.finish()
+    conv_y.finish()
 
     rows2 = c2.shape[0] // 3
     wide = w1.shape[1]
@@ -387,15 +461,24 @@
             even[part],
             odd[part, 16 : 16 + count, :].astype(BF16),
         )
+        at = slice(2 * part, 2 * part + 2)
+        blocks = (
+            c2y[at, :, 0:rows2, :],
+            jnp.concatenate([c2y[at, :, rows2:BY_Y, :], c2f[at, :, 0 : 2 * rows2 - BY_Y, :]], axis=2),
+            c2f[at, :, 2 * rows2 - BY_Y :, :],
+        )
         for tap in range(3):
-            w = c2f[2 * part : 2 * part + 2, :, tap * rows2 : (tap + 1) * rows2, :].reshape(4 * rows2, wide)
+            w = blocks[tap].reshape(4 * rows2, wide)
             second = second + jnp.dot(taps[tap], w, preferred_element_type=F32)
     hbox[me] = gelu(second).astype(BF16)
     share_h = Across(hbox.at[me], hbox, hb_s, hb_r)
     share_h.start()
-    qkv.step(1)
+    for k in (5, 6, 7):
+        qkv_y.pass_on(k)
+    kvw.arrive(1)
+    kvw.arrive(2)
     share_h.relay()
-    qkv.step(2)
+    kvw.pass_on(0)
     own_g.wait()
     gains.finish()
     share_h.finish()
@@ -405,14 +488,14 @@
     inv = lax.rsqrt(sum(jnp.sum(p * p, axis=1, keepdims=True) for p in parts) / D + 1e-05)
     for k in range(4):
         nbuf[k] = (parts[k] * inv * gf[k, 0:1, :]).astype(BF16)
-    qkv.step(3)
-    kvw.begin()
-    qkv.step(Z // 2)
-    qkv.finish()
+    qkv_y.finish()
+    qkv_z.finish()
     projected = jnp.zeros((count, qw.shape[1]), F32)
     for k in range(4):
         projected = projected + jnp.dot(
-            nbuf[k], qwf[2 * k : 2 * k + 2].reshape(4 * qw.shape[0], qw.shape[1]), preferred_element_type=F32
+            nbuf[k], jnp.concatenate(
+                [qwy[2 * k : 2 * k + 2], qwz[2 * k : 2 * k + 2]], axis=2
+            ).reshape(4 * qw.shape[0], qw.shape[1]), preferred_element_type=F32
         )
     split = count // 2
     lower = lax.broadcasted_iota(jnp.int32, (split, 128), 1) < HD
@@ -459,14 +542,18 @@
             pltpu.make_async_copy(pk.at[i, 0:half], kv.at[z, c, rows], loc.at[0]).wait()
             pltpu.make_async_copy(pk.at[i, half:], qbox.at[i], loc.at[1]).wait()
 
+    width = kv.shape[2]
+
     def block(ref_z, core):
         return kv.at[ref_z, core]
 
     def send_up(t, zz):
-        return remote(block(zz, c), block(zz, c), up_s.at[t], up_r.at[t], up)
+        ref = block(zz, c) if t < Z // 2 - 1 else kv.at[zz, c, pl.ds(0, width // 2)]
+        return remote(ref, ref, up_s.at[t], up_r.at[t], up)
 
     def send_down(t, zz):
-        return remote(block(zz, c), block(zz, c), dn_s.at[t], dn_r.at[t], down)
+        ref = block(zz, c) if t < Z // 2 - 1 else kv.at[zz, c, pl.ds(width // 2, width // 2)]
+        return remote(ref, ref, dn_s.at[t], dn_r.at[t], down)
 
     def share(k, zz):
         return remote(block(zz, c), block(zz, c), co_s.at[k], co_r.at[k], twin)
@@ -488,73 +575,87 @@
         ).astype(BF16)
 
     total = qs.shape[0]
-    width = kv.shape[2]
-
     def process(zz, core):
-        def tile(k, carry):
-            rows = pl.ds(pl.multiple_of(k * TQ, TQ), TQ)
-            pairs = kv[zz, core]
-            s = lax.dot_general(
-                qs[rows, :], pairs, (((1,), (1,)), ((), ())), preferred_element_type=F32
-            )
-            old = m[rows, :]
-            new = jnp.maximum(old, jnp.max(s, axis=1, keepdims=True))
-            m[rows, :] = new
-            decay = jnp.exp(old - new)
-            w = jnp.exp(s - jnp.concatenate([new] * (width // 128), axis=1))
-            part = w[:, 0:128]
-            for piece in range(1, width // 128):
-                part = part + w[:, piece * 128 : (piece + 1) * 128]
-            l[rows, :] = l[rows, :] * decay + part
-            acc[rows, :] = acc[rows, :] * decay + jnp.dot(
-                w.astype(BF16), pairs, preferred_element_type=F32
-            )
+        pairs = kv[zz, core]
+        s = lax.dot_general(qs[...], pairs, (((1,), (1,)), ((), ())), preferred_element_type=F32)
+        old = m[...]
+        new = jnp.maximum(old, jnp.max(s, axis=1, keepdims=True))
+        m[...] = new
+        decay = jnp.exp(old - new)
+        w = jnp.exp(s - jnp.concatenate([new] * (width // 128), axis=1))
+        part = w[:, 0:128]
+        for piece in range(1, width // 128):
+            part = part + w[:, piece * 128 : (piece + 1) * 128]
+        l[...] = l[...] * decay + part
+        acc[...] = acc[...] * decay + jnp.dot(w.astype(BF16), pairs, preferred_element_type=F32)
+
+    def both(zz, other, core):
+        def turn(i, carry):
+            process(jnp.where(i == 0, zz, other), core)
             return carry
 
-        lax.fori_loop(0, total // TQ, tile, 0)
-
+        lax.fori_loop(0, 2, turn, 0)
+
+    kvw.pass_on(1)
+    kvw.pass_on(2)
     process(z, c)
     taken(0, z).wait_recv()
     process(z, 1 - c)
     far = Z // 2
-    kvw.pass_on(0)
     for t in range(1, far + 1):
         below = lax.rem(z + Z - t, Z)
         above = lax.rem(z + t, Z)
         send_up(t - 1, below).wait_recv()
         if t < far:
             send_up(t, below).start()
-        share(2 * t - 1, below).start()
+            share(2 * t - 1, below).start()
+        send_down(t - 1, above).wait_recv()
         if t < far:
-            send_down(t - 1, above).wait_recv()
-            if t < far - 1:
-                send_down(t, above).start()
+            send_down(t, above).start()
             share(2 * t, above).start()
-        process(below, c)
-        kvw.arrive(2 * t - 1)
+        else:
+            share(2 * t - 1, below).start()
+        if t == 1:
+            kvw.arrive(3)
+            kvw.arrive(4)
         if t < far:
-            kvw.arrive(2 * t)
-        if t > 1:
-            kvw.pass_on(2 * t - 3)
-            kvw.pass_on(2 * t - 2)
-        if t < far:
-            process(above, c)
+            both(below, above, c)
+        else:
+            process(below, c)
         if t == 1:
-            proj.start()
+            for k in (1, 2):
+                proj_y.arrive(k)
+                proj_z.arrive(k)
+        if t == 2:
+            kvw.arrive(5)
+            kvw.arrive(6)
+            for k in (3, 4):
+                proj_y.arrive(k)
+                proj_z.arrive(k)
+            proj_y.pass_on(0)
+        if t == 3:
+            for k in (5, 6):
+                proj_y.arrive(k)
+                proj_z.arrive(k)
+            kvw.arrive(7)
+            outw.relay()
         taken(2 * t - 1, below).wait_recv()
-        process(below, 1 - c)
-        if t == 2:
-            proj.start_other()
-            outw.relay()
-        if t == 3:
-            proj.step(1)
         if t < far:
             taken(2 * t, above).wait_recv()
-            process(above, 1 - c)
+            both(below, above, 1 - c)
+        else:
+            process(below, 1 - c)
+        if t == 2:
+            kvw.pass_on(3)
+            kvw.pass_on(4)
+            proj_y.pass_on(1)
+            proj_y.pass_on(2)
         if t == 3:
-            proj.step(2)
-        if t == 4:
-            proj.step(3)
+            proj_y.arrive(7)
+            proj_z.arrive(7)
+            proj_y.pass_on(3)
+            proj_y.pass_on(4)
+            kvw.pass_on(5)
 
     quarter = half // 4
     low = lax.broadcasted_iota(jnp.int32, (quarter // 2, 128), 1) < HD
@@ -584,12 +685,12 @@
             def _():
                 pltpu.make_async_copy(obuf.at[4 * j + q], abox.at[head], loc.at[0]).start()
 
-    proj.step(far)
-    kvw.pass_on(2 * far - 1)
+    for k in (5, 6, 7):
+        proj_y.pass_on(k)
+    kvw.pass_on(6)
 
     for t in range(far):
         send_up(t, z).wait_send()
-    for t in range(far - 1):
         send_down(t, z).wait_send()
     for k in range(2 * far):
         share(k, z).wait_send()
@@ -633,12 +734,16 @@
     gather = Across(pbox.at[me], pbox, pb_s, pb_r)
     gather.start()
     gather.relay()
-    proj.finish()
+    kvw.pass_on(7)
+    proj_y.finish()
+    proj_z.finish()
     gather.finish()
 
     post = pbox[...].reshape(4 * tokens, pbox.shape[2])
     embedded = jnp.dot(
-        post, pwf[...].reshape(2 * Z * pw.shape[0], pw.shape[1]), preferred_element_type=F32
+        post,
+        jnp.concatenate([pwy[...], pwz[...]], axis=2).reshape(2 * Z * pw.shape[0], pw.shape[1]),
+        preferred_element_type=F32,
     ).astype(BF16)
     widened = embedded.astype(F32)
     sbox[me] = jnp.broadcast_to(
@@ -646,45 +751,74 @@
     )
     squares = Across(sbox.at[me], sbox, sb_s, sb_r)
     squares.start()
-    gained = (widened * rg[0:1, :]).astype(BF16)
-    cols = pw.shape[1]
-    kvw.finish()
-
-    def columns(a, b):
-        at = pl.ds(pl.multiple_of((a * 2 + b) * cols, cols), cols)
-        return jnp.dot(
-            gained, kwf[:, :, :, :, at].reshape(cols, cols), preferred_element_type=F32
-        )
+    ebox[x_lo] = (widened * rg[0:1, :]).astype(BF16)
+    side = device(y, x_hi, c, z, 1 - x_lo)
+
+    def lend(b):
+        return remote(ebox.at[b], ebox.at[b], e_s.at[0], e_r.at[0], side)
+
+    def hand(src):
+        return remote(src, precv, e_s.at[1], e_r.at[1], side)
 
     def swap(k):
         return remote(tsend.at[k], trecv.at[k], t_s.at[k], t_r.at[k], twin)
 
-    over = remote(csend, crecv, c_s.at[0], c_r.at[0], far_dev)
-    tsend[0] = columns(1 - x_hi, 1 - c).astype(BF16)
-    swap(0).start()
-    keep[...] = columns(1 - x_hi, c)
-    squares.relay()
-    swap(0).wait_recv()
-    csend[...] = (keep[...] + trecv[0].astype(F32)).astype(BF16)
-    over.start()
-    tsend[1] = columns(x_hi, 1 - c).astype(BF16)
-    swap(1).start()
-    keep[...] = columns(x_hi, c)
+    def over(k):
+        return remote(csend.at[k], crecv.at[k], c_s.at[k], c_r.at[k], far_dev)
+
+    lend(x_lo).start()
+    kvw.finish()
+    cols = pw.shape[1]
+    part_c = cols // 2
+
+    def columns(rows, a, b):
+        at = pl.ds(pl.multiple_of((a * 2 + b) * part_c, part_c), part_c)
+        return jnp.dot(ebox[rows], kwf[:, :, :, at].reshape(cols, part_c), preferred_element_type=F32)
+
+    for k in range(2):
+        rows = x_lo if k == 0 else 1 - x_lo
+        if k == 1:
+            lend(rows).wait_recv()
+        tsend[k, 0] = columns(rows, 1 - x_hi, 1 - c).astype(BF16)
+        tsend[k, 1] = columns(rows, x_hi, 1 - c).astype(BF16)
+        swap(k).start()
+        keep[k, 0] = columns(rows, 1 - x_hi, c)
+        keep[k, 1] = columns(rows, x_hi, c)
+        if k == 0:
+            squares.relay()
+        swap(k).wait_recv()
+        csend[k] = (keep[k, 0] + trecv[k, 0].astype(F32)).astype(BF16)
+        over(k).start()
+        keep[k, 1] = keep[k, 1] + trecv[k, 1].astype(F32)
     squares.finish()
     scale = lax.rsqrt((sbox[0] + sbox[1] + sbox[2] + sbox[3]) / DL + 1e-06)
-    swap(1).wait_recv()
-    keep[...] = keep[...] + trecv[1].astype(F32)
-    over.wait_recv()
-    for h in range(cols // LHD):
+
+    def turned(value, h, base):
+        value = value * scale
+        at = pl.ds(pl.multiple_of(base + h * LHD, LHD), LHD)
+        out[:, at] = (value * cs[...] + pltpu.roll(value, HD, 1) * sn[...]).astype(BF16)
+
+    heads_half = part_c // LHD
+    over(0).wait_recv()
+    for h in range(heads_half):
         at = slice(h * LHD, (h + 1) * LHD)
-        value = (keep[:, at] + crecv[:, at].astype(F32)) * scale
-        out[:, at] = (value * cs[...] + pltpu.roll(value, HD, 1) * sn[...]).astype(BF16)
-
+        turned(keep[0, 1, :, at] + crecv[0, :, at].astype(F32), h, x_lo * part_c)
+    over(1).wait_recv()
+    psend[...] = (keep[1, 1] + crecv[1].astype(F32)).astype(BF16)
+    hand(psend).start()
+    hand(psend).wait_recv()
+    for h in range(heads_half):
+        at = slice(h * LHD, (h + 1) * LHD)
+        turned(precv[:, at].astype(F32), h, (1 - x_lo) * part_c)
+
+    lend(x_lo).wait_send()
+    hand(psend).wait_send()
+    over(1).wait_send()
     edge_next.wait_send()
     edge_prev.wait_send()
     swap(0).wait_send()
     swap(1).wait_send()
-    over.wait_send()
+    over(0).wait_send()
     for j in range(n):
         for q in range(4):
             own = jnp.logical_and(mirror, jnp.logical_and(y == j, me == q))
@@ -711,15 +845,18 @@
     return pl.pallas_call(
         layer_kernel,
         out_shape=jax.ShapeDtypeStruct((tokens, cols), BF16),
-        in_specs=[vm] * 11,
+        in_specs=[vm] * 7 + [pl.BlockSpec(memory_space=pl.ANY)] + [vm] * 3,
         out_specs=vm,
         scratch_shapes=[
             V((16, mel.shape[1]), BF16),
             V((16, mel.shape[1]), BF16),
             V((4,) + w1.shape, BF16),
             V((4,) + gn.shape, F32),
-            V((Z, 2) + c2.shape, BF16),
-            V((Z, 2) + qw.shape, BF16),
+            V((Z, 2, c2.shape[0] - BY_Y, wide), BF16),
+            V((Z, 2, BY_Y, wide), BF16),
+            V((Z, 2, ROWS_Y, qw.shape[1]), BF16),
+            V((Z, 2, qw.shape[0] - ROWS_Y, qw.shape[1]), BF16),
+            V((2, kw.shape[0], kw.shape[1] // 2), BF16),
             V((frames + 32, mel.shape[1]), F32),
             V((4, frames, wide), BF16),
             V((4, frames + 16, wide), F32),
@@ -737,22 +874,27 @@
             V((quarter, ow.shape[0] * 4), BF16),
             V((ow.shape[1] // 128, quarter, 128), F32),
             V((4,) + ow.shape, BF16),
-            V((Z, 2) + pw.shape, BF16),
-            V((Z, 2) + kw.shape, BF16),
+            V((Z, 2, ROWS_Y, cols), BF16),
+            V((Z, 2, pw.shape[0] - ROWS_Y, cols), BF16),
+            V((Z, 2, kw.shape[0], kw.shape[1] // 2), BF16),
             V((4, quarter // 2, ow.shape[1]), BF16),
             V((4, tokens, 128), F32),
-            V((tokens, cols), F32),
             V((2, tokens, cols), BF16),
-            V((2, tokens, cols), BF16),
-            V((tokens, cols), BF16),
-            V((tokens, cols), BF16),
-            sem((n,)), sem((n,)), sem((n,)), sem((n,)), sem((10,)),
+            V((2, 2, tokens, cols // 2), F32),
+            V((2, 2, tokens, cols // 2), BF16),
+            V((2, 2, tokens, cols // 2), BF16),
+            V((2, tokens, cols // 2), BF16),
+            V((2, tokens, cols // 2), BF16),
+            V((tokens, cols // 2), BF16),
+            V((tokens, cols // 2), BF16),
+            sem((n,)), sem((n,)), sem((n,)), sem((n,)), sem((20,)),
             sem((half,)), sem((half,)), sem((half,)), sem((half,)), sem((Z,)), sem((Z,)), sem((16,)), sem((16,)),
-            sem((3,)), sem((3,)), sem((3,)), sem((3,)), sem((3,)), sem((3,)), sem((2,)), sem((2,)), sem((1,)), sem((1,)),
+            sem((3,)), sem((3,)), sem((3,)), sem((3,)), sem((3,)), sem((3,)), sem((2,)), sem((2,)), sem((2,)), sem((2,)), sem((2,)), sem((2,)),
             sem((2,)), sem((2,)), sem((3,)), sem((3,)), sem((3,)), sem((3,)), sem((3,)), sem((3,)),
         ]
-        + ring * 3
-        + [sem((half,))] * 4 + [sem((1,))] * 2 + [sem((Z,))] * 8,
+        + ring
+        + ([sem((half,))] * 4 + [sem((1,))] * 2 + [sem((Z,))] * 8) * 4
+        + ([sem((half,))] * 4 + [sem((1,))] * 2) * 2,
         compiler_params=pltpu.CompilerParams(
             collective_id=1, has_side_effects=True, vmem_limit_bytes=60 * 2**20
         ),
@@ -799,7 +941,7 @@
         weight,
         out_weight,
         proj_weight,
-        kv_weight.reshape(4, kv_weight.shape[0] // 4, kv_weight.shape[1]),
+        kv_weight,
         rms_gain.reshape(1, -1),
         cs,
         sn,

time: 187 us -> 155 us (0.83)
  Pallas kernels: 179 us -> 147 us
    pallas_call x1, Pallas kernels: 179 us -> 147 us  [layer(): pl.pallas_call(layer_kernel, out_shape=jax.ShapeDtypeStruct((tokens, cols...]
where the time goes in v4:
time: 155 us; the launch traced here: 154 us
  Pallas kernels  147 us (95%)
  local copies, waits for them, and re-layouts  5.37 us (3%)
  other arithmetic  2.27 us (1%)
    pallas_call x1, Pallas kernels, layer(): pl.pallas_call(layer_kernel, out_shape=jax.ShapeDtypeStruct((tokens, cols...  147 us
    unnamed x13, local copies, waits for them, and re-layouts  3.76 us

profile of v4, /device:TPU:1, one launch (start us, length us, event | category | flops | bytes accessed | tf_op | source)
XLA Modules:
  0.0 154.4 jit_solution(1100649549741950732)
XLA Ops:
  0.0 0.0 copy-start.3
  0.0 0.0 copy-start.4
  0.0 0.0 copy-start.2
  0.0 0.6 copy-done.3
  0.7 0.0 copy-done.4
  0.7 0.6 select_maximum_fusion.gn
  1.3 0.8 slice_bitcast_fusion.2
  2.1 1.0 fusion.2
  3.1 0.0 copy-done.2
  3.1 0.0 copy-start.1
  3.1 0.7 reshape.40.mel
  3.8 0.2 copy-done.1
  4.0 0.2 copy.14
  4.2 0.0 copy-start
  4.2 0.1 copy.17
  4.3 0.7 pad_maximum_fusion.1.qw
  5.0 0.2 copy-done
  5.2 0.9 copy.13
  6.0 146.7 %shard_map.100 = bf16[128,1024]{1,0:T(8,128)(2,1)} custom-call(bf16[256,256]{1,0:T(8,128)(2,1)} %reshape.40.mel, bf16[384,320]{1,0:T(8,128)(2,1)} %bitcast.13, bf16[240,320]{1,0:T(8,128)(2,1)} %bitcast.16, f32[8,320]{1,0:T(8,128)} %select_maximum_fusion.gn, bf16[80,768]{1,0:T(8,128)(2,1)} %pad_maximum_fusion.1.qw, bf16[256,1280]{1,0:T(8,128)(2,1)} %ow.1, ...), custom_call_target="tpu_custom_call" | custom-call | tf_op jit(solution)/shard_map/pallas_call | solution.py:845
  152.8 1.7 %copy.19 = bf16[128,1024]{1,0:T(8,128)(2,1)} copy(bf16[128,1024]{1,0:T(8,128)(2,1)} %shard_map.100) | data formatting | bytes 524288
  (7 shorter events, 0.1 us)
Async XLA Ops:
  0.0 0.7 copy-start.3
  0.0 0.7 copy-start.4
  0.0 3.1 %copy-start.2 = (bf16[512,128]{1,0:T(8,128)(2,1)S(1)}, bf16[512,128]{1,0:T(8,128)(2,1)}, u32[]{:S(2)}) copy-start(bf16[512,128]{1,0:T(8,128)(2,1)} %param.10) | copy-start | bytes 393220
  3.1 0.9 copy-start.1
  4.2 0.9 copy-start

commit v5 on v4

--- a/solution.py
+++ b/solution.py
@@ -104,7 +104,7 @@
         self.src, self.buf, self.z, self.x = src, buf, z, x_lo
         self.s = (us, ur, ds, dr, ous, our, ods, odr, xs, xr)
         self.loc = loc
-        self.lo = pl.ds(0, h0)
+        self.h0 = h0
         self.hi = pl.ds(h0, src.shape[0] - h0)
         self.up = device(y, x_hi, c, lax.rem(z + 1, self.Z), x_lo)
         self.down = device(y, x_hi, c, lax.rem(z + self.Z - 1, self.Z), x_lo)
@@ -118,16 +118,18 @@
 
     def ring(self, kind, t, zz, src=None):
         us, ur, ds, dr, ous, our, ods, odr, xs, xr = self.s
-        if kind == "u":
-            ref = self.buf.at[zz, self.x]
-            return remote(ref if src is None else src, ref, us.at[t], ur.at[t], self.up)
-        if kind == "d":
-            ref = self.buf.at[zz, self.x]
-            return remote(ref if src is None else src, ref, ds.at[t], dr.at[t], self.down)
-        ref = self.buf.at[zz, 1 - self.x, self.lo]
-        if kind == "ou":
-            return remote(ref, ref, ous.at[t], our.at[t], self.up)
-        return remote(ref, ref, ods.at[t], odr.at[t], self.down)
+        own = kind in "ud"
+        count = self.src.shape[0] if own else self.h0
+        cut = (count // 2 + 15) // 16 * 16
+        if t < self.Z // 2 - 1:
+            rows = pl.ds(0, count)
+        else:
+            rows = pl.ds(0, cut) if kind[-1] == "u" else pl.ds(cut, count - cut)
+        ref = self.buf.at[zz, self.x if own else 1 - self.x, rows]
+        send, recv, to = {
+            "u": (us, ur, self.up), "d": (ds, dr, self.down), "ou": (ous, our, self.up), "od": (ods, odr, self.down)
+        }[kind]
+        return remote(ref if src is None else src, ref, send.at[t], recv.at[t], to)
 
     def whole(self, x):
         us, ur, ds, dr, ous, our, ods, odr, xs, xr = self.s
@@ -154,29 +156,17 @@
 
     def step(self, t):
         far = self.Z // 2
-        zz = self.below(t)
-        self.ring("u", t - 1, zz).wait_recv()
-        if t < far:
-            self.ring("u", t, zz).start()
-        self.forward(2 * t - 1, zz, self.x).start()
-        if t < far:
-            zz = self.above(t)
-            self.ring("d", t - 1, zz).wait_recv()
-            if t < far - 1:
-                self.ring("d", t, zz).start()
-            self.forward(2 * t, zz, self.x).start()
-        self.step_other(t)
-
-    def step_other(self, t):
-        far = self.Z // 2
-        zz = self.below(t)
-        self.ring("ou", t - 1, zz).wait_recv()
-        if t < far:
-            self.ring("ou", t, zz).start()
-            zz = self.above(t)
-            self.ring("od", t - 1, zz).wait_recv()
-            if t < far - 1:
-                self.ring("od", t, zz).start()
+        for kind, zz, k in (("u", self.below(t), 2 * t - 1), ("d", self.above(t), 2 * t)):
+            self.ring(kind, t - 1, zz).wait_recv()
+            if t < far:
+                self.ring(kind, t, zz).start()
+                self.forward(k, zz, self.x).start()
+        if t == far:
+            self.forward(2 * t - 1, self.below(t), self.x).start()
+        for kind, zz in (("ou", self.below(t)), ("od", self.above(t))):
+            self.ring(kind, t - 1, zz).wait_recv()
+            if t < far:
+                self.ring(kind, t, zz).start()
 
     def finish(self):
         far = self.Z // 2
@@ -187,11 +177,8 @@
         self.local().wait()
         self.whole(self.x).wait_send()
         for t in range(far):
-            self.ring("u", t, self.z).wait_send()
-            self.ring("ou", t, self.z).wait_send()
-        for t in range(far - 1):
-            self.ring("d", t, self.z).wait_send()
-            self.ring("od", t, self.z).wait_send()
+            for kind in ("u", "d", "ou", "od"):
+                self.ring(kind, t, self.z).wait_send()
         for k in range(1, 2 * far):
             self.forward(k, self.z, self.x).wait_send()
 
@@ -224,7 +211,8 @@
 
     def ring(self, kind, t, zz):
         us, ur, ds, dr = self.s[:4]
-        ref = self.buf.at[zz, :, self.part(self.y)]
+        shard = slice(None) if t < self.Z // 2 - 1 else (0 if kind == "u" else 1)
+        ref = self.buf.at[zz, shard, self.part(self.y)]
         if kind == "u":
             return remote(ref, ref, us.at[t], ur.at[t], self.up)
         return remote(ref, ref, ds.at[t], dr.at[t], self.down)
@@ -269,16 +257,17 @@
             self.spread("p", 0, self.y).start()
 
     def fetch(self, k):
-        self.ring("u" if k % 2 else "d", (k + 1) // 2 - 1, self.zs(k)).wait_recv()
+        last = (k + 1) // 2 == self.Z // 2
+        for kind in "ud" if last else ("u" if k % 2 else "d"):
+            self.ring(kind, (k + 1) // 2 - 1, self.zs(k)).wait_recv()
         if self.Y > 1:
             self.spread("n", k, self.y).start()
             self.spread("p", k, self.y).start()
 
     def onward(self, k):
-        far, t = self.Z // 2, (k + 1) // 2
-        kind = "u" if k % 2 else "d"
-        if t < (far if kind == "u" else far - 1):
-            self.ring(kind, t, self.zs(k)).start()
+        t = (k + 1) // 2
+        if t < self.Z // 2:
+            self.ring("u" if k % 2 else "d", t, self.zs(k)).start()
 
     def arrive(self, k):
         self.fetch(k)
@@ -301,7 +290,6 @@
         self.cross(self.x).wait_send()
         for t in range(far):
             self.ring("u", t, self.z).wait_send()
-        for t in range(far - 1):
             self.ring("d", t, self.z).wait_send()
         for k in turns:
             self.spread("n", k, self.y).wait_send()
@@ -322,7 +310,7 @@
     hprev, hnext, w1f, gf, c2f, c2y, qwy, qwz, kwa, xe, even, odd, hbox, nbuf, pk,
     kv, qbox, qs, m, l, acc, obuf, abox, att, res, owf, pwy, pwz, kwf, pbox, sbox, ebox, keep, tsend, trecv, csend, crecv, psend, precv,
     kv_s, kv_r, q_s, q_r, loc, up_s, up_r, dn_s, dn_r, co_s, co_r, a_s, a_r,
-    ow_s, ow_r, pb_s, pb_r, sb_s, sb_r, t_s, t_r, c_s, c_r, e_s, e_r,
+    ow_s, ow_r, pb_s, pb_r, sb_s, sb_r, t_s, t_r, c_s, c_r, e_s, e_r, pc_s, pc_r,
     h_s, h_r, w1_s, w1_r, g_s, g_r, hb_s, hb_r,
     *rings,
 ):
@@ -438,19 +426,19 @@
     conv_y.pass_on(4)
     qkv_y.pass_on(1)
     qkv_y.pass_on(2)
-    kvw.begin()
     conv_y.arrive(7)
     conv.step(Z // 2)
     qkv_y.arrive(7)
     qkv_z.arrive(7)
     for k in (5, 6, 7):
         conv_y.pass_on(k)
+    kvw.begin()
     qkv_y.pass_on(3)
     qkv_y.pass_on(4)
+    conv.finish()
+    conv_y.finish()
     proj_y.begin()
     proj_z.begin()
-    conv.finish()
-    conv_y.finish()
 
     rows2 = c2.shape[0] // 3
     wide = w1.shape[1]
@@ -685,9 +673,6 @@
             def _():
                 pltpu.make_async_copy(obuf.at[4 * j + q], abox.at[head], loc.at[0]).start()
 
-    for k in (5, 6, 7):
-        proj_y.pass_on(k)
-    kvw.pass_on(6)
 
     for t in range(far):
         send_up(t, z).wait_send()
@@ -730,32 +715,40 @@
             (res.at[k][pl.ds(0, tokens, stride=2), :] + res.at[k][pl.ds(1, tokens, stride=2), :]) * 0.5
         )
     pooled = jnp.concatenate(pieces, axis=1)
-    pbox[me] = normal(pooled, gain).astype(BF16)
-    gather = Across(pbox.at[me], pbox, pb_s, pb_r)
+    pbox[x_lo, me] = normal(pooled, gain).astype(BF16)
+    side = device(y, x_hi, c, z, 1 - x_lo)
+
+    def lend(b):
+        return remote(pbox.at[b, me], pbox.at[b, me], e_s.at[0], e_r.at[0], side)
+
+    lend(x_lo).start()
+    gather = Across(pbox.at[x_lo, me], pbox.at[x_lo], pb_s, pb_r)
     gather.start()
+    lend(1 - x_lo).wait_recv()
+    beside = Across(pbox.at[1 - x_lo, me], pbox.at[1 - x_lo], pc_s, pc_r)
+    beside.start()
+    for k in (5, 6, 7):
+        proj_y.pass_on(k)
     gather.relay()
+    kvw.pass_on(6)
     kvw.pass_on(7)
     proj_y.finish()
     proj_z.finish()
     gather.finish()
 
-    post = pbox[...].reshape(4 * tokens, pbox.shape[2])
-    embedded = jnp.dot(
-        post,
-        jnp.concatenate([pwy[...], pwz[...]], axis=2).reshape(2 * Z * pw.shape[0], pw.shape[1]),
-        preferred_element_type=F32,
-    ).astype(BF16)
-    widened = embedded.astype(F32)
+    def embed(b):
+        post = pbox[b].reshape(4 * tokens, pbox.shape[3])
+        weight = jnp.concatenate([pwy[...], pwz[...]], axis=2).reshape(2 * Z * pw.shape[0], pw.shape[1])
+        return jnp.dot(post, weight, preferred_element_type=F32).astype(BF16).astype(F32)
+
+    widened = embed(x_lo)
     sbox[me] = jnp.broadcast_to(
         jnp.sum(widened * widened, axis=1, keepdims=True), (4 * tokens, 128)
     )
     squares = Across(sbox.at[me], sbox, sb_s, sb_r)
     squares.start()
     ebox[x_lo] = (widened * rg[0:1, :]).astype(BF16)
-    side = device(y, x_hi, c, z, 1 - x_lo)
-
-    def lend(b):
-        return remote(ebox.at[b], ebox.at[b], e_s.at[0], e_r.at[0], side)
+    beside.relay()
 
     def hand(src):
         return remote(src, precv, e_s.at[1], e_r.at[1], side)
@@ -766,7 +759,6 @@
     def over(k):
         return remote(csend.at[k], crecv.at[k], c_s.at[k], c_r.at[k], far_dev)
 
-    lend(x_lo).start()
     kvw.finish()
     cols = pw.shape[1]
     part_c = cols // 2
@@ -778,7 +770,8 @@
     for k in range(2):
         rows = x_lo if k == 0 else 1 - x_lo
         if k == 1:
-            lend(rows).wait_recv()
+            beside.finish()
+            ebox[rows] = (embed(rows) * rg[0:1, :]).astype(BF16)
         tsend[k, 0] = columns(rows, 1 - x_hi, 1 - c).astype(BF16)
         tsend[k, 1] = columns(rows, x_hi, 1 - c).astype(BF16)
         swap(k).start()
@@ -877,7 +870,7 @@
             V((Z, 2, ROWS_Y, cols), BF16),
             V((Z, 2, pw.shape[0] - ROWS_Y, cols), BF16),
             V((Z, 2, kw.shape[0], kw.shape[1] // 2), BF16),
-            V((4, quarter // 2, ow.shape[1]), BF16),
+            V((2, 4, quarter // 2, ow.shape[1]), BF16),
             V((4, tokens, 128), F32),
             V((2, tokens, cols), BF16),
             V((2, 2, tokens, cols // 2), F32),
@@ -889,7 +882,7 @@
             V((tokens, cols // 2), BF16),
             sem((n,)), sem((n,)), sem((n,)), sem((n,)), sem((20,)),
             sem((half,)), sem((half,)), sem((half,)), sem((half,)), sem((Z,)), sem((Z,)), sem((16,)), sem((16,)),
-            sem((3,)), sem((3,)), sem((3,)), sem((3,)), sem((3,)), sem((3,)), sem((2,)), sem((2,)), sem((2,)), sem((2,)), sem((2,)), sem((2,)),
+            sem((3,)), sem((3,)), sem((3,)), sem((3,)), sem((3,)), sem((3,)), sem((2,)), sem((2,)), sem((2,)), sem((2,)), sem((2,)), sem((2,)), sem((3,)), sem((3,)),
             sem((2,)), sem((2,)), sem((3,)), sem((3,)), sem((3,)), sem((3,)), sem((3,)), sem((3,)),
         ]
         + ring

time: 155 us -> 151 us (0.974)
  Pallas kernels: 147 us -> 142 us
    pallas_call x1, Pallas kernels: 147 us -> 142 us  [layer(): pl.pallas_call(layer_kernel, out_shape=jax.ShapeDtypeStruct((tokens, cols...]
where the time goes in v5:
time: 151 us; the launch traced here: 150 us
  Pallas kernels  142 us (94%)
  local copies, waits for them, and re-layouts  5.37 us (4%)
  other arithmetic  2.27 us (2%)
    pallas_call x1, Pallas kernels, layer(): pl.pallas_call(layer_kernel, out_shape=jax.ShapeDtypeStruct((tokens, cols...  142 us
    unnamed x13, local copies, waits for them, and re-layouts  3.76 us

profile of v5, /device:TPU:1, one launch (start us, length us, event | category | flops | bytes accessed | tf_op | source)
XLA Modules:
  0.0 149.9 jit_solution(12582960691890175435)
XLA Ops:
  0.0 0.0 copy-start.3
  0.0 0.0 copy-start.4
  0.0 0.0 copy-start.2
  0.0 0.6 copy-done.3
  0.7 0.0 copy-done.4
  0.7 0.6 select_maximum_fusion.gn
  1.3 0.8 slice_bitcast_fusion.2
  2.1 1.0 fusion.2
  3.1 0.0 copy-done.2
  3.1 0.0 copy-start.1
  3.1 0.7 reshape.40.mel
  3.8 0.2 copy-done.1
  4.0 0.2 copy.14
  4.2 0.0 copy-start
  4.2 0.1 copy.17
  4.3 0.7 pad_maximum_fusion.1.qw
  5.0 0.2 copy-done
  5.2 0.9 copy.13
  6.0 142.1 %shard_map.100 = bf16[128,1024]{1,0:T(8,128)(2,1)} custom-call(bf16[256,256]{1,0:T(8,128)(2,1)} %reshape.40.mel, bf16[384,320]{1,0:T(8,128)(2,1)} %bitcast.13, bf16[240,320]{1,0:T(8,128)(2,1)} %bitcast.16, f32[8,320]{1,0:T(8,128)} %select_maximum_fusion.gn, bf16[80,768]{1,0:T(8,128)(2,1)} %pad_maximum_fusion.1.qw, bf16[256,1280]{1,0:T(8,128)(2,1)} %ow.1, ...), custom_call_target="tpu_custom_call" | custom-call | tf_op jit(solution)/shard_map/pallas_call | solution.py:838
  148.2 1.7 %copy.19 = bf16[128,1024]{1,0:T(8,128)(2,1)} copy(bf16[128,1024]{1,0:T(8,128)(2,1)} %shard_map.100) | data formatting | bytes 524288
  (7 shorter events, 0.1 us)
Async XLA Ops:
  0.0 0.7 copy-start.3
  0.0 0.7 copy-start.4
  0.0 3.1 %copy-start.2 = (bf16[512,128]{1,0:T(8,128)(2,1)S(1)}, bf16[512,128]{1,0:T(8,128)(2,1)}, u32[]{:S(2)}) copy-start(bf16[512,128]{1,0:T(8,128)(2,1)} %param.10) | copy-start | bytes 393220
  3.1 0.9 copy-start.1
  4.2 0.9 copy-start
